TPU v7x, 32 devices: a whole 2x2x4 slice. The times are simulated.
32 devices in a mesh: groups: 2 (over x), seq: 16 (over z, y, core).
Axes of the slice: x: 2, y: 2, z: 4, core: 2. Of those that a mesh axis runs over, the one named last changes fastest.
Arguments:
- q_fresh: bfloat16 [5120, 4096], P(('groups', 'seq')), parts along dimension 0, may hold values from -9 to 9, as said below
- k_fresh: bfloat16 [5120, 4096], P(('groups', 'seq')), parts along dimension 0, may hold values from -5.6 to 5.6, as said below
- v_fresh: bfloat16 [5120, 4096], P(('groups', 'seq')), parts along dimension 0, may hold values from -6 to 6
- k_stale: bfloat16 [5120, 4096], P('groups', 'seq'), parts along dimension 0, may hold values from -5.59375 to 5.59375
- v_stale: bfloat16 [5120, 4096], P('groups', 'seq'), parts along dimension 0, may hold values from -6 to 6
- rank: int32 [10], P('groups'), parts along dimension 0, may hold values from 0 to 4, each once
- ends: int32 [10], P('groups'), parts along dimension 0, may hold values from 512 to 2560, as said below
Outputs:
- attended: bfloat16 [5120, 4096], P(('groups', 'seq')), parts along dimension 0
There are 2 independent parts, one for each index of `groups`. A program takes and returns all parts, laid end to end along the dimension named above; each array names one. Nothing has to cross between parts.
Inputs may be any that keep to these rules, and one draw needn't show every extreme that they name: `q_fresh`: queries of both draws lie within this range. `k_fresh`: keys of both draws lie within this range. Multiples of 512, never falling along the patches, ends[p] >= (p + 1) * 512; the first equals 512, the last equals 2560.
All inputs are finite; a program needn't handle non-finite values.
Results may differ from a plain program's by a relative error of at most 0.0036.
Values may be sent and summed in bfloat16 or wider, within the bound.
No kernel may reach another device: no remote copies, remote signals or barrier semaphores. Data moves between devices by JAX's collectives and lax.ppermute only.
A program may use at most 64 MiB of HBM per device.

v0:
```python
import math

import jax
import jax.numpy as jnp
from jax import lax
from jax.sharding import PartitionSpec as P

HEAD_DIM = 128
PATCH = 512


def shards(q_fresh, k_fresh, v_fresh, k_stale, v_stale, rank, ends):
    queries, keys_new, values_new = (
        lax.all_to_all(q_fresh, "seq", split_axis=1, concat_axis=0, tiled=True),
        lax.all_to_all(k_fresh, "seq", split_axis=1, concat_axis=0, tiled=True),
        lax.all_to_all(v_fresh, "seq", split_axis=1, concat_axis=0, tiled=True),
    )
    total_rows = queries.shape[0]
    width = queries.shape[1]
    heads_here = width // HEAD_DIM
    patch_count = rank.shape[0]
    scale = 1.0 / math.sqrt(HEAD_DIM)
    key_patch = jnp.arange(total_rows, dtype=jnp.int32) // PATCH
    hits = key_patch[:, None] == jnp.arange(patch_count, dtype=jnp.int32)[None, :]
    key_rank = jnp.sum(jnp.where(hits, rank[None, :], 0), axis=1)
    positions = jnp.arange(total_rows, dtype=jnp.int32)

    def split_heads(array):
        return array.reshape(array.shape[0], heads_here, HEAD_DIM)

    def one_patch(index):
        block = split_heads(lax.dynamic_slice_in_dim(queries, index * PATCH, PATCH, 0))
        my_rank = rank[index]
        limit = ends[index]
        fresh = (key_rank <= my_rank)[:, None]
        keys = split_heads(jnp.where(fresh, keys_new, k_stale))
        values = split_heads(jnp.where(fresh, values_new, v_stale))
        score = jnp.einsum("qhd,khd->hqk", block, keys, preferred_element_type=jnp.float32) * scale
        score = jnp.where((positions < limit)[None, None, :], score, -jnp.inf)
        top = jnp.max(score, axis=2, keepdims=True)
        weight = jnp.exp(score - top)
        denominator = jnp.sum(weight, axis=2)
        mixed = jnp.einsum(
            "hqk,khd->qhd", weight.astype(jnp.bfloat16), values, preferred_element_type=jnp.float32
        )
        result = mixed / jnp.transpose(denominator)[:, :, None]
        return result.reshape(PATCH, width).astype(jnp.bfloat16)

    pieces = lax.map(one_patch, jnp.arange(patch_count, dtype=jnp.int32))
    gathered = pieces.reshape(total_rows, width)
    return lax.all_to_all(gathered, "seq", split_axis=0, concat_axis=1, tiled=True)


def solution(mesh):
    return jax.shard_map(
        shards,
        mesh=mesh,
        in_specs=(
            P(("groups", "seq"), None),
            P(("groups", "seq"), None),
            P(("groups", "seq"), None),
            P("groups", "seq"),
            P("groups", "seq"),
            P("groups"),
            P("groups"),
        ),
        out_specs=P(("groups", "seq"), None),
        check_vma=False,
    )
```

profile of v0, /device:TPU:1, one launch (start us, length us, event | category | flops | bytes accessed | tf_op | source)
XLA Modules:
  0.0 222.0 jit_solution(114587770779463893)
XLA Ops:
  0.0 2.5 %copy.83 = bf16[20,16,8,256]{3,2,0,1:T(8,128)(2,1)} copy(bf16[20,16,8,256]{3,2,1,0:T(8,128)(2,1)} %bitcast.75) | data formatting | bytes 2621440 | tf_op jit(solution)/shard_map/all_to_all | solution.py:16
  2.5 7.5 %all-to-all-start = ((bf16[160,16,256]{2,0,1:T(8,128)(2,1)}), bf16[160,16,256]{2,0,1:T(8,128)(2,1)S(1)}, u32[]{:S(2)}, u32[]{:S(2)}) async-start(bf16[160,16,256]{2,0,1:T(8,128)(2,1)} %bitcast.41), calls=%async_computation | async-start | bytes 2621440 | tf_op jit(solution)/shard_map/all_to_all | solution.py:16
  10.0 1.2 copy.81
  11.2 26.6 %all-to-all-done = bf16[160,16,256]{2,0,1:T(8,128)(2,1)S(1)} async-done(((bf16[160,16,256]{2,0,1:T(8,128)(2,1)}), bf16[160,16,256]{2,0,1:T(8,128)(2,1)S(1)}, u32[]{:S(2)}, u32[]{:S(2)}) %all-to-all-start) | async-done | bytes 1310752 | tf_op jit(solution)/shard_map/all_to_all | solution.py:16
  37.8 7.5 %all-to-all-start.2 = ((bf16[160,16,256]{2,0,1:T(8,128)(2,1)}), bf16[160,16,256]{2,0,1:T(8,128)(2,1)S(1)}, u32[]{:S(2)}, u32[]{:S(2)}) async-start(bf16[160,16,256]{2,0,1:T(8,128)(2,1)} %bitcast.73), calls=%async_computation.2 | async-start | bytes 2621440 | tf_op jit(solution)/shard_map/all_to_all | solution.py:15
  45.3 2.5 %copy.82 = bf16[20,16,8,256]{3,2,0,1:T(8,128)(2,1)} copy(bf16[20,16,8,256]{3,2,1,0:T(8,128)(2,1)} %bitcast.77) | data formatting | bytes 2621440 | tf_op jit(solution)/shard_map/all_to_all | solution.py:14
  47.8 25.3 %all-to-all-done.2 = bf16[160,16,256]{2,0,1:T(8,128)(2,1)S(1)} async-done(((bf16[160,16,256]{2,0,1:T(8,128)(2,1)}), bf16[160,16,256]{2,0,1:T(8,128)(2,1)S(1)}, u32[]{:S(2)}, u32[]{:S(2)}) %all-to-all-start.2) | async-done | bytes 1310752 | tf_op jit(solution)/shard_map/all_to_all | solution.py:15
  73.1 1.1 copy-done
  74.2 7.5 %all-to-all-start.1 = ((bf16[160,16,256]{2,0,1:T(8,128)(2,1)}), bf16[160,16,256]{2,0,1:T(8,128)(2,1)}, u32[]{:S(2)}, u32[]{:S(2)}) async-start(bf16[160,16,256]{2,0,1:T(8,128)(2,1)} %bitcast.72), calls=%async_computation.1 | async-start | bytes 2621440 | tf_op jit(solution)/shard_map/all_to_all | solution.py:14
  81.7 2.4 %copy.63 = bf16[2560,256]{0,1:T(8,128)(2,1)} copy(bf16[2560,256]{1,0:T(8,128)(2,1)} %param.13) | data formatting | bytes 2621440
  84.1 1.6 copy.66
  85.9 1.6 copy.62
  87.5 1.6 copy.65
  89.1 20.6 %all-to-all-done.1 = bf16[160,16,256]{2,0,1:T(8,128)(2,1)} async-done(((bf16[160,16,256]{2,0,1:T(8,128)(2,1)}), bf16[160,16,256]{2,0,1:T(8,128)(2,1)}, u32[]{:S(2)}, u32[]{:S(2)}) %all-to-all-start.1) | async-done | bytes 1310752 | tf_op jit(solution)/shard_map/all_to_all | solution.py:14
  109.6 71.8 %while.11 = (s32[]{:T(128)}, bf16[5,512,256]{2,1,0:T(8,128)(2,1)}, s32[5]{0:T(128)S(1)}, s32[5]{0:T(128)S(1)}, s32[2560]{0:T(1024)S(1)}, /*index=5*/bf16[2560,25...) while((s32[]{:T(128)}, bf16[5,512,256]{2,1,0:T(8,128)(2,1)}, ...), condition=%wide.region_4.5_spmd.clone, body=%wide.region_1.4_spmd.clone.sunk | while | flops 1372589056 | bytes 49856844 | solution.py:49
  112.1 0.7 dynamic_slice.24
  113.4 1.3 iota_compare_fusion.3
  115.3 1.0 constant_dynamic-slice_fusion.2
  116.4 1.7 fusion.43
  118.2 2.2 %fusion.44 = f32[2,512]{1,0:T(2,128)S(1)} fusion(f32[2,512,2560]{2,1,0:T(8,128)S(1)} %get-tuple-element.257, f32[2,512]{1,0:T(2,128)S(1)} %get-tuple-element.258, pred[2560]{0:T(1024)(128)(4,1)S(1)} %get-tuple-element.255), kind=kLoop, calls=%fused_computation.4.clone.1 | loop fusion | flops 10484736 | bytes 10496512 | tf_op jit(solution)/shard_map/while/body/eval_jaxpr/reduce_sum | solution.py:42
  120.4 2.7 %fusion.45 = bf16[512,2,128]{0,2,1:T(8,128)(2,1)S(1)} fusion(f32[2,512,2560]{2,1,0:T(8,128)S(1)} %get-tuple-element.257, f32[2,512]{1,0:T(2,128)S(1)} %get-tuple-element.258, pred[2560]{0:T(1024)(128)(4,1)S(1)} %get-tuple-element.255, bf16[2560,2,128]{0,2,1:T(8,128)(2,1)S(1)} %bitcast.79, bf16[2560,2,128]{0,2,1:T(8,128)(2,1)S(1)} %bitcast.78, ...), kind=kOutput, calls=%fused_computation.15.clone.1 | convolution fusion | flops 682491904 | bytes 13382656 | tf_op jit(solution)/shard_map/while/body/eval_jaxpr/hqk,khd->qhd/dot_general | solution.py:43
  123.3 0.7 constant_dynamic-update-slice_fusion.2
  127.8 1.3 iota_compare_fusion.3
  129.7 1.0 constant_dynamic-slice_fusion.2
  130.8 1.7 fusion.43
  132.5 2.2 %fusion.44 = f32[2,512]{1,0:T(2,128)S(1)} fusion(f32[2,512,2560]{2,1,0:T(8,128)S(1)} %get-tuple-element.257, f32[2,512]{1,0:T(2,128)S(1)} %get-tuple-element.258, pred[2560]{0:T(1024)(128)(4,1)S(1)} %get-tuple-element.255), kind=kLoop, calls=%fused_computation.4.clone.1 | loop fusion | flops 10484736 | bytes 10496512 | tf_op jit(solution)/shard_map/while/body/eval_jaxpr/reduce_sum | solution.py:42
  134.8 2.7 %fusion.45 = bf16[512,2,128]{0,2,1:T(8,128)(2,1)S(1)} fusion(f32[2,512,2560]{2,1,0:T(8,128)S(1)} %get-tuple-element.257, f32[2,512]{1,0:T(2,128)S(1)} %get-tuple-element.258, pred[2560]{0:T(1024)(128)(4,1)S(1)} %get-tuple-element.255, bf16[2560,2,128]{0,2,1:T(8,128)(2,1)S(1)} %bitcast.79, bf16[2560,2,128]{0,2,1:T(8,128)(2,1)S(1)} %bitcast.78, ...), kind=kOutput, calls=%fused_computation.15.clone.1 | convolution fusion | flops 682491904 | bytes 13382656 | tf_op jit(solution)/shard_map/while/body/eval_jaxpr/hqk,khd->qhd/dot_general | solution.py:43
  137.7 0.7 constant_dynamic-update-slice_fusion.2
  142.1 1.3 iota_compare_fusion.3
  144.0 1.0 constant_dynamic-slice_fusion.2
  145.2 1.7 fusion.43
  146.9 2.2 %fusion.44 = f32[2,512]{1,0:T(2,128)S(1)} fusion(f32[2,512,2560]{2,1,0:T(8,128)S(1)} %get-tuple-element.257, f32[2,512]{1,0:T(2,128)S(1)} %get-tuple-element.258, pred[2560]{0:T(1024)(128)(4,1)S(1)} %get-tuple-element.255), kind=kLoop, calls=%fused_computation.4.clone.1 | loop fusion | flops 10484736 | bytes 10496512 | tf_op jit(solution)/shard_map/while/body/eval_jaxpr/reduce_sum | solution.py:42
  149.2 2.7 %fusion.45 = bf16[512,2,128]{0,2,1:T(8,128)(2,1)S(1)} fusion(f32[2,512,2560]{2,1,0:T(8,128)S(1)} %get-tuple-element.257, f32[2,512]{1,0:T(2,128)S(1)} %get-tuple-element.258, pred[2560]{0:T(1024)(128)(4,1)S(1)} %get-tuple-element.255, bf16[2560,2,128]{0,2,1:T(8,128)(2,1)S(1)} %bitcast.79, bf16[2560,2,128]{0,2,1:T(8,128)(2,1)S(1)} %bitcast.78, ...), kind=kOutput, calls=%fused_computation.15.clone.1 | convolution fusion | flops 682491904 | bytes 13382656 | tf_op jit(solution)/shard_map/while/body/eval_jaxpr/hqk,khd->qhd/dot_general | solution.py:43
  152.0 0.7 constant_dynamic-update-slice_fusion.2
  156.5 1.3 iota_compare_fusion.3
  158.4 1.0 constant_dynamic-slice_fusion.2
  159.5 1.7 fusion.43
  161.3 2.2 %fusion.44 = f32[2,512]{1,0:T(2,128)S(1)} fusion(f32[2,512,2560]{2,1,0:T(8,128)S(1)} %get-tuple-element.257, f32[2,512]{1,0:T(2,128)S(1)} %get-tuple-element.258, pred[2560]{0:T(1024)(128)(4,1)S(1)} %get-tuple-element.255), kind=kLoop, calls=%fused_computation.4.clone.1 | loop fusion | flops 10484736 | bytes 10496512 | tf_op jit(solution)/shard_map/while/body/eval_jaxpr/reduce_sum | solution.py:42
  163.5 2.7 %fusion.45 = bf16[512,2,128]{0,2,1:T(8,128)(2,1)S(1)} fusion(f32[2,512,2560]{2,1,0:T(8,128)S(1)} %get-tuple-element.257, f32[2,512]{1,0:T(2,128)S(1)} %get-tuple-element.258, pred[2560]{0:T(1024)(128)(4,1)S(1)} %get-tuple-element.255, bf16[2560,2,128]{0,2,1:T(8,128)(2,1)S(1)} %bitcast.79, bf16[2560,2,128]{0,2,1:T(8,128)(2,1)S(1)} %bitcast.78, ...), kind=kOutput, calls=%fused_computation.15.clone.1 | convolution fusion | flops 682491904 | bytes 13382656 | tf_op jit(solution)/shard_map/while/body/eval_jaxpr/hqk,khd->qhd/dot_general | solution.py:43
  166.4 0.7 constant_dynamic-update-slice_fusion.2
  170.9 1.3 iota_compare_fusion.3
  172.8 1.0 constant_dynamic-slice_fusion.2
  173.9 1.7 fusion.43
  175.6 2.2 %fusion.44 = f32[2,512]{1,0:T(2,128)S(1)} fusion(f32[2,512,2560]{2,1,0:T(8,128)S(1)} %get-tuple-element.257, f32[2,512]{1,0:T(2,128)S(1)} %get-tuple-element.258, pred[2560]{0:T(1024)(128)(4,1)S(1)} %get-tuple-element.255), kind=kLoop, calls=%fused_computation.4.clone.1 | loop fusion | flops 10484736 | bytes 10496512 | tf_op jit(solution)/shard_map/while/body/eval_jaxpr/reduce_sum | solution.py:42
  177.9 2.7 %fusion.45 = bf16[512,2,128]{0,2,1:T(8,128)(2,1)S(1)} fusion(f32[2,512,2560]{2,1,0:T(8,128)S(1)} %get-tuple-element.257, f32[2,512]{1,0:T(2,128)S(1)} %get-tuple-element.258, pred[2560]{0:T(1024)(128)(4,1)S(1)} %get-tuple-element.255, bf16[2560,2,128]{0,2,1:T(8,128)(2,1)S(1)} %bitcast.79, bf16[2560,2,128]{0,2,1:T(8,128)(2,1)S(1)} %bitcast.78, ...), kind=kOutput, calls=%fused_computation.15.clone.1 | convolution fusion | flops 682491904 | bytes 13382656 | tf_op jit(solution)/shard_map/while/body/eval_jaxpr/hqk,khd->qhd/dot_general | solution.py:43
  180.8 0.7 constant_dynamic-update-slice_fusion.2
  181.5 39.3 %all_to_all.76 = bf16[16,160,256]{2,1,0:T(8,128)(2,1)S(1)} all-to-all(bf16[16,160,256]{2,1,0:T(8,128)(2,1)} %bitcast.80), channel_id=1, replica_groups=mesh['groups'=2,'seq'=16] {'seq'}, dimensions={0} | all-to-all | bytes 2621440 | tf_op jit(solution)/shard_map/all_to_all | solution.py:51
  220.8 1.2 copy.77
  (55 shorter events, 10.4 us)
Async XLA Ops:
  2.5 7.5 %copy-start.1 = (bf16[160,4096]{1,0:T(8,128)(2,1)S(1)}, bf16[160,4096]{1,0:T(8,128)(2,1)}, u32[]{:S(2)}) copy-start(bf16[160,4096]{1,0:T(8,128)(2,1)} %param.10) | copy-start | bytes 3932164
  2.5 35.3 %all-to-all-start = ((bf16[160,16,256]{2,0,1:T(8,128)(2,1)}), bf16[160,16,256]{2,0,1:T(8,128)(2,1)S(1)}, u32[]{:S(2)}, u32[]{:S(2)}) async-start(bf16[160,16,256]{2,0,1:T(8,128)(2,1)} %bitcast.41), calls=%async_computation | async-start | bytes 2621440 | tf_op jit(solution)/shard_map/all_to_all | solution.py:16
  37.8 35.3 %all-to-all-start.2 = ((bf16[160,16,256]{2,0,1:T(8,128)(2,1)}), bf16[160,16,256]{2,0,1:T(8,128)(2,1)S(1)}, u32[]{:S(2)}, u32[]{:S(2)}) async-start(bf16[160,16,256]{2,0,1:T(8,128)(2,1)} %bitcast.73), calls=%async_computation.2 | async-start | bytes 2621440 | tf_op jit(solution)/shard_map/all_to_all | solution.py:15
  73.1 1.1 copy-start
  74.2 35.4 %all-to-all-start.1 = ((bf16[160,16,256]{2,0,1:T(8,128)(2,1)}), bf16[160,16,256]{2,0,1:T(8,128)(2,1)}, u32[]{:S(2)}, u32[]{:S(2)}) async-start(bf16[160,16,256]{2,0,1:T(8,128)(2,1)} %bitcast.72), calls=%async_computation.1 | async-start | bytes 2621440 | tf_op jit(solution)/shard_map/all_to_all | solution.py:14
  84.1 1.6 copy-start.4
  87.5 22.2 %copy-start.5 = (s32[5]{0:T(128)S(1)}, s32[5]{0:T(128)}, u32[]{:S(2)}) copy-start(s32[5]{0:T(128)} %param.15) | copy-start | bytes 64
  118.1 2.3 %copy-start.2 = (bf16[2560,256]{0,1:T(8,128)(2,1)S(1)}, bf16[2560,256]{0,1:T(8,128)(2,1)}, u32[]{:S(2)}) copy-start(bf16[2560,256]{0,1:T(8,128)(2,1)} %get-tuple-element.297) | copy-start | bytes 3932164 | tf_op jit(solution)/shard_map/while
  118.2 2.3 %copy-start.3 = (bf16[2560,256]{0,1:T(8,128)(2,1)S(1)}, bf16[2560,256]{0,1:T(8,128)(2,1)}, u32[]{:S(2)}) copy-start(bf16[2560,256]{0,1:T(8,128)(2,1)} %get-tuple-element.296) | copy-start | bytes 3932164 | tf_op jit(solution)/shard_map/while
  132.5 2.3 %copy-start.2 = (bf16[2560,256]{0,1:T(8,128)(2,1)S(1)}, bf16[2560,256]{0,1:T(8,128)(2,1)}, u32[]{:S(2)}) copy-start(bf16[2560,256]{0,1:T(8,128)(2,1)} %get-tuple-element.297) | copy-start | bytes 3932164 | tf_op jit(solution)/shard_map/while
  132.5 2.3 %copy-start.3 = (bf16[2560,256]{0,1:T(8,128)(2,1)S(1)}, bf16[2560,256]{0,1:T(8,128)(2,1)}, u32[]{:S(2)}) copy-start(bf16[2560,256]{0,1:T(8,128)(2,1)} %get-tuple-element.296) | copy-start | bytes 3932164 | tf_op jit(solution)/shard_map/while
  146.9 2.3 %copy-start.2 = (bf16[2560,256]{0,1:T(8,128)(2,1)S(1)}, bf16[2560,256]{0,1:T(8,128)(2,1)}, u32[]{:S(2)}) copy-start(bf16[2560,256]{0,1:T(8,128)(2,1)} %get-tuple-element.297) | copy-start | bytes 3932164 | tf_op jit(solution)/shard_map/while
  146.9 2.3 %copy-start.3 = (bf16[2560,256]{0,1:T(8,128)(2,1)S(1)}, bf16[2560,256]{0,1:T(8,128)(2,1)}, u32[]{:S(2)}) copy-start(bf16[2560,256]{0,1:T(8,128)(2,1)} %get-tuple-element.296) | copy-start | bytes 3932164 | tf_op jit(solution)/shard_map/while
  161.3 2.3 %copy-start.2 = (bf16[2560,256]{0,1:T(8,128)(2,1)S(1)}, bf16[2560,256]{0,1:T(8,128)(2,1)}, u32[]{:S(2)}) copy-start(bf16[2560,256]{0,1:T(8,128)(2,1)} %get-tuple-element.297) | copy-start | bytes 3932164 | tf_op jit(solution)/shard_map/while
  161.3 2.3 %copy-start.3 = (bf16[2560,256]{0,1:T(8,128)(2,1)S(1)}, bf16[2560,256]{0,1:T(8,128)(2,1)}, u32[]{:S(2)}) copy-start(bf16[2560,256]{0,1:T(8,128)(2,1)} %get-tuple-element.296) | copy-start | bytes 3932164 | tf_op jit(solution)/shard_map/while
  175.6 2.3 %copy-start.2 = (bf16[2560,256]{0,1:T(8,128)(2,1)S(1)}, bf16[2560,256]{0,1:T(8,128)(2,1)}, u32[]{:S(2)}) copy-start(bf16[2560,256]{0,1:T(8,128)(2,1)} %get-tuple-element.297) | copy-start | bytes 3932164 | tf_op jit(solution)/shard_map/while
  175.6 2.3 %copy-start.3 = (bf16[2560,256]{0,1:T(8,128)(2,1)S(1)}, bf16[2560,256]{0,1:T(8,128)(2,1)}, u32[]{:S(2)}) copy-start(bf16[2560,256]{0,1:T(8,128)(2,1)} %get-tuple-element.296) | copy-start | bytes 3932164 | tf_op jit(solution)/shard_map/while
where the time goes:
time: 223 us; the launch traced here: 222 us
  waiting for transfers between devices  72.5 us (33%)
  blocking collectives  39.3 us (18%)
  local copies, waits for them, and re-layouts  35.2 us (16%)
  starting transfers between devices  22.4 us (10%)
  matrix products  22.2 us (10%)
  other arithmetic  17.6 us (8%)
  loops' own time  12.7 us (6%)
    all_to_all x1, blocking collectives, shards(): lax.all_to_all(gathered, 'seq', split_axis=0, concat_axis=1, tiled=True)  39.3 us
    all_to_all x1, waiting for transfers between devices, shards(): lax.all_to_all(v_fresh, 'seq', split_axis=1, concat_axis=0, tiled=True)  26.6 us
    all_to_all x1, waiting for transfers between devices, shards(): lax.all_to_all(k_fresh, 'seq', split_axis=1, concat_axis=0, tiled=True)  25.3 us
    all_to_all x1, waiting for transfers between devices, shards(): lax.all_to_all(q_fresh, 'seq', split_axis=1, concat_axis=0, tiled=True)  20.6 us
    dot_general x5, matrix products, one_patch(): jnp.einsum('hqk,khd->qhd', weight.astype(jnp.bfloat16), values, preferred...  13.6 us
    another operation x1, loops' own time, shards(): pieces = lax.map(one_patch, jnp.arange(patch_count, dtype=jnp.int32))  12.7 us
    reduce_sum x5, other arithmetic, one_patch(): denominator = jnp.sum(weight, axis=2)  11.2 us
    dot_general x5, matrix products, one_patch(): jnp.einsum('qhd,khd->hqk', block, keys, preferred_element_type=jnp.float32)  8.59 us
  transfers between devices with their start and end apart: 3, of which 3 were waited for; matrix products, arithmetic and copies ran while one was open for 5% of the time, Pallas kernels for 0%

commit v1 on v0

v1 whole, which is shorter than its diff:
```python
import functools
import math

import jax
import jax.numpy as jnp
from jax import lax
from jax.experimental import pallas as pl
from jax.experimental.pallas import tpu as pltpu
from jax.sharding import PartitionSpec as P

HEAD_DIM = 128
PATCH = 512


def attend_kernel(rank_ref, ends_ref, q_ref, kf_ref, vf_ref, ks_ref, vs_ref, out_ref, *, scale):
    p = pl.program_id(0)
    mine = rank_ref[p]
    count = ends_ref[p] // PATCH
    rows = q_ref.shape[0] * q_ref.shape[1]
    flat = (rows, HEAD_DIM)
    query = q_ref.reshape(*flat)[pl.ds(pl.multiple_of(p * PATCH, PATCH), PATCH), :]
    keys_new = kf_ref.reshape(*flat)
    values_new = vf_ref.reshape(*flat)

    def step(j, carry):
        top, total, mixed = carry
        at = pl.ds(pl.multiple_of(j * PATCH, PATCH), PATCH)
        fresh = rank_ref[j] <= mine
        keys = jnp.where(fresh, keys_new[at, :], ks_ref[at, :])
        values = jnp.where(fresh, values_new[at, :], vs_ref[at, :])
        score = lax.dot_general(query, keys, (((1,), (1,)), ((), ())), preferred_element_type=jnp.float32) * scale
        higher = jnp.maximum(top, jnp.max(score, axis=1, keepdims=True))
        weight = jnp.exp(score - higher)
        shrink = jnp.exp(top - higher)
        total = total * shrink + jnp.sum(weight, axis=1, keepdims=True)
        mixed = mixed * shrink + jnp.dot(weight.astype(jnp.bfloat16), values, preferred_element_type=jnp.float32)
        return higher, total, mixed

    start = (
        jnp.full((PATCH, 1), -jnp.inf, jnp.float32),
        jnp.zeros((PATCH, 1), jnp.float32),
        jnp.zeros((PATCH, HEAD_DIM), jnp.float32),
    )
    _, total, mixed = lax.fori_loop(0, count, step, start)
    out_ref[...] = (mixed / total).astype(jnp.bfloat16)


def attend(packed, k_stale, v_stale, rank, ends, head):
    shards_here, _, rows_here, _ = packed.shape
    total_rows = shards_here * rows_here
    part = [
        pl.BlockSpec((shards_here, None, rows_here, HEAD_DIM), lambda p, r, e, i=i: (0, i, 0, 0))
        for i in range(3)
    ]
    stale = pl.BlockSpec((total_rows, HEAD_DIM), lambda p, r, e: (0, head))
    return pl.pallas_call(
        functools.partial(attend_kernel, scale=1.0 / math.sqrt(HEAD_DIM)),
        grid_spec=pltpu.PrefetchScalarGridSpec(
            num_scalar_prefetch=2,
            grid=(rank.shape[0],),
            in_specs=[*part, stale, stale],
            out_specs=pl.BlockSpec((PATCH, HEAD_DIM), lambda p, r, e: (p, 0)),
        ),
        out_shape=jax.ShapeDtypeStruct((total_rows, HEAD_DIM), jnp.bfloat16),
        name="attend",
    )(rank, ends, packed, packed, packed, k_stale, v_stale)


def pack_kernel(q_ref, k_ref, v_ref, out_ref, *, head, heads_here):
    for t in range(out_ref.shape[0]):
        at = (t * heads_here + head) * HEAD_DIM
        for i, ref in enumerate((q_ref, k_ref, v_ref)):
            out_ref[t, i] = ref[:, at:at + HEAD_DIM]


def pack(arrays, others, heads_here, head):
    rows_here = arrays[0].shape[0]
    each = math.gcd(others, 4)
    wide = each * heads_here * HEAD_DIM
    return pl.pallas_call(
        functools.partial(pack_kernel, head=head, heads_here=heads_here),
        grid=(others // each,),
        in_specs=[pl.BlockSpec((rows_here, wide), lambda g: (0, g))] * 3,
        out_specs=pl.BlockSpec((each, 3, rows_here, HEAD_DIM), lambda g: (g, 0, 0, 0)),
        out_shape=jax.ShapeDtypeStruct((others, 3, rows_here, HEAD_DIM), jnp.bfloat16),
        name="pack",
    )(*arrays)


def unpack_kernel(*refs):
    out_ref = refs[-1]
    heads_here = len(refs) - 1
    for head in range(heads_here):
        for t in range(refs[head].shape[0]):
            at = (t * heads_here + head) * HEAD_DIM
            out_ref[:, at:at + HEAD_DIM] = refs[head][t]


def unpack(returned):
    heads_here = len(returned)
    others, rows_here, _ = returned[0].shape
    each = math.gcd(others, 4)
    return pl.pallas_call(
        unpack_kernel,
        grid=(others // each,),
        in_specs=[pl.BlockSpec((each, rows_here, HEAD_DIM), lambda g: (g, 0, 0))] * heads_here,
        out_specs=pl.BlockSpec((rows_here, each * heads_here * HEAD_DIM), lambda g: (0, g)),
        out_shape=jax.ShapeDtypeStruct((rows_here, others * heads_here * HEAD_DIM), jnp.bfloat16),
        name="unpack",
    )(*returned)


def shards(q_fresh, k_fresh, v_fresh, k_stale, v_stale, rank, ends):
    heads_here = k_stale.shape[1] // HEAD_DIM
    others = q_fresh.shape[1] // k_stale.shape[1]
    rows_here = q_fresh.shape[0]
    arrived = []
    for head in range(heads_here):
        packed = pack((q_fresh, k_fresh, v_fresh), others, heads_here, head)
        arrived.append(lax.all_to_all(packed, "seq", split_axis=0, concat_axis=0, tiled=True))
    returned = []
    for head in range(heads_here):
        result = attend(arrived[head], k_stale, v_stale, rank, ends, head)
        result = result.reshape(others, rows_here, HEAD_DIM)
        returned.append(lax.all_to_all(result, "seq", split_axis=0, concat_axis=0, tiled=True))
    return unpack(returned)


def solution(mesh):
    return jax.shard_map(
        shards,
        mesh=mesh,
        in_specs=(
            P(("groups", "seq"), None),
            P(("groups", "seq"), None),
            P(("groups", "seq"), None),
            P("groups", "seq"),
            P("groups", "seq"),
            P("groups"),
            P("groups"),
        ),
        out_specs=P(("groups", "seq"), None),
        check_vma=False,
    )
```

time: 223 us -> 158 us (0.71)
  Pallas kernels: 0 us -> 47.4 us
  local copies, waits for them, and re-layouts: 35.2 us -> 1.28 us
  matrix products: 22.2 us -> 0 us
  other arithmetic: 17.6 us -> 0 us
  waiting for transfers between devices: 72.5 us -> 56.6 us
  blocking collectives: 39.3 us -> 24.2 us
  loops' own time: 12.7 us -> 0 us
  starting transfers between devices: 22.4 us -> 27.6 us
    pallas_call x0 -> x5, Pallas kernels: none -> 47.4 us  [the longest x2 35.4 us: attend(): pl.pallas_call(functools.partial(attend_kernel, scale=1.0 / math.sqrt(HEA...]
    dot_general x10 -> x0, matrix products: 22.2 us -> none  [the longest x5 13.6 us: one_patch(): jnp.einsum('hqk,khd->qhd', weight.astype(jnp.bfloat16), values, preferred...]
    all_to_all x3, waiting for transfers between devices: 72.5 us -> 56.6 us  [the longest x2 56.6 us: shards(): lax.all_to_all(packed, 'seq', split_axis=0, concat_axis=0, tiled=True)]
    all_to_all x1, blocking collectives: 39.3 us -> 24.2 us  [shards(): lax.all_to_all(result, 'seq', split_axis=0, concat_axis=0, tiled=True)]
    dynamic_slice x25 -> x0, local copies, waits for them, and re-layouts: 15.1 us -> none  [the longest x10 5.57 us: one_patch(): lax.dynamic_slice_in_dim(queries, index * PATCH, PATCH, 0)]
    another operation x1 -> x0, loops' own time: 12.7 us -> none  [shards(): pieces = lax.map(one_patch, jnp.arange(patch_count, dtype=jnp.int32))]
    reduce_sum x6 -> x0, other arithmetic: 11.3 us -> none  [the longest x5 11.2 us: one_patch(): denominator = jnp.sum(weight, axis=2)]
    all_to_all x4 -> x0, local copies, waits for them, and re-layouts: 7.42 us -> none  [the longest x1 2.51 us: shards(): lax.all_to_all(v_fresh, 'seq', split_axis=1, concat_axis=0, tiled=True)]
  transfers between devices with their start and end apart: 3 -> 3, of which waited for: 3 -> 2; matrix products, arithmetic and copies ran while one was open for 5% -> 0% of each run, Pallas kernels for 0% -> 25%
where the time goes in v1:
time: 158 us; the launch traced here: 157 us
  waiting for transfers between devices  56.6 us (36%)
  Pallas kernels  47.4 us (30%)
  starting transfers between devices  27.6 us (17%)
  blocking collectives  24.2 us (15%)
    all_to_all x2, waiting for transfers between devices, shards(): lax.all_to_all(packed, 'seq', split_axis=0, concat_axis=0, tiled=True)  56.6 us
    pallas_call x2, Pallas kernels, attend(): pl.pallas_call(functools.partial(attend_kernel, scale=1.0 / math.sqrt(HEA...  35.4 us
    all_to_all x1, blocking collectives, shards(): lax.all_to_all(result, 'seq', split_axis=0, concat_axis=0, tiled=True)  24.2 us
    all_to_all x2, starting transfers between devices, shards(): lax.all_to_all(packed, 'seq', split_axis=0, concat_axis=0, tiled=True)  17.5 us
    all_to_all x1, starting transfers between devices, shards(): lax.all_to_all(result, 'seq', split_axis=0, concat_axis=0, tiled=True)  10.1 us
    pallas_call x2, Pallas kernels, pack(): pl.pallas_call(functools.partial(pack_kernel, head=head, heads_here=heads...  8.34 us
    pallas_call x1, Pallas kernels, unpack(): pl.pallas_call(unpack_kernel, grid=(others // each,), in_specs=[pl.BlockS...  3.65 us
  transfers between devices with their start and end apart: 3, of which 2 were waited for; matrix products, arithmetic and copies ran while one was open for 0% of the time, Pallas kernels for 25%

profile of v1, /device:TPU:1, one launch (start us, length us, event | category | flops | bytes accessed | tf_op | source)
XLA Modules:
  0.0 157.1 jit_solution(15887775899922242374)
XLA Ops:
  0.0 4.2 %pack.3 = bf16[16,3,160,128]{3,2,1,0:T(8,128)(2,1)} custom-call(bf16[160,4096]{1,0:T(8,128)(2,1)} %q_ref.3, bf16[160,4096]{1,0:T(8,128)(2,1)} %k_ref.3, bf16[160,4096]{1,0:T(8,128)(2,1)} %v_ref.3), custom_call_target="tpu_custom_call" | custom-call | tf_op jit(solution)/shard_map/pack/pallas_call | solution.py:80
  4.2 7.3 %all-to-all-start.2 = ((bf16[16,3,160,128]{3,2,1,0:T(8,128)(2,1)}), bf16[16,3,160,128]{3,2,1,0:T(8,128)(2,1)S(1)}, u32[]{:S(2)}, u32[]{:S(2)}) async-start(bf16[16,3,160,128]{3,2,1,0:T(8,128)(2,1)} %pack.3), calls=%async_computation.2 | async-start | bytes 3932160 | tf_op jit(solution)/shard_map/all_to_all | solution.py:120
  11.5 4.2 %pack.2 = bf16[16,3,160,128]{3,2,1,0:T(8,128)(2,1)} custom-call(bf16[160,4096]{1,0:T(8,128)(2,1)} %q_ref.3, bf16[160,4096]{1,0:T(8,128)(2,1)} %k_ref.3, bf16[160,4096]{1,0:T(8,128)(2,1)} %v_ref.3), custom_call_target="tpu_custom_call" | custom-call | tf_op jit(solution)/shard_map/pack/pallas_call | solution.py:80
  15.7 35.1 %all-to-all-done.2.q_ref.kf_ref.vf_ref = bf16[16,3,160,128]{3,2,1,0:T(8,128)(2,1)S(1)} async-done(((bf16[16,3,160,128]{3,2,1,0:T(8,128)(2,1)}), bf16[16,3,160,128]{3,2,1,0:T(8,128)(2,1)S(1)}, u32[]{:S(2)}, u32[]{:S(2)}) %all-to-all-start.2) | async-done | bytes 1966112 | tf_op jit(solution)/shard_map/all_to_all | solution.py:120
  50.7 0.0 copy-start.1
  50.8 1.3 copy-done.1
  52.0 10.1 %all-to-all-start = ((bf16[16,3,160,128]{3,2,1,0:T(8,128)(2,1)}), bf16[16,3,160,128]{3,2,1,0:T(8,128)(2,1)S(1)}, u32[]{:S(2)}, u32[]{:S(2)}) async-start(bf16[16,3,160,128]{3,2,1,0:T(8,128)(2,1)} %pack.2), calls=%async_computation | async-start | bytes 3932160 | tf_op jit(solution)/shard_map/all_to_all | solution.py:120
  62.2 17.7 %attend.3 = bf16[2560,128]{1,0:T(8,128)(2,1)} custom-call(s32[5]{0:T(128)} %rank_ref.3, s32[5]{0:T(128)} %ends_ref.3, bf16[16,3,160,128]{3,2,1,0:T(8,128)(2,1)} %copy-done.1, bf16[16,3,160,128]{3,2,1,0:T(8,128)(2,1)} %copy-done.1, bf16[16,3,160,128]{3,2,1,0:T(8,128)(2,1)} %copy-done.1, bf16[2560,256]{1,0:T(8,128)(2,1)} %ks_ref.3, bf16[2560,256]{1,0:T(8,128)(2,1)} %vs_ref.3), custom_call_target="tpu_custom_call" | custom-call | tf_op jit(solution)/shard_map/attend/pallas_call | solution.py:56
  79.9 21.5 %all-to-all-done.q_ref.kf_ref.vf_ref = bf16[16,3,160,128]{3,2,1,0:T(8,128)(2,1)S(1)} async-done(((bf16[16,3,160,128]{3,2,1,0:T(8,128)(2,1)}), bf16[16,3,160,128]{3,2,1,0:T(8,128)(2,1)S(1)}, u32[]{:S(2)}, u32[]{:S(2)}) %all-to-all-start) | async-done | bytes 1966112 | tf_op jit(solution)/shard_map/all_to_all | solution.py:120
  101.4 0.0 copy-start
  101.4 10.1 %all-to-all-start.3 = ((bf16[16,160,128]{2,1,0:T(8,128)(2,1)}), bf16[16,160,128]{2,1,0:T(8,128)(2,1)S(1)}, u32[]{:S(2)}, u32[]{:S(2)}) async-start(bf16[16,160,128]{2,1,0:T(8,128)(2,1)} %bitcast.2), calls=%async_computation.3 | async-start | bytes 1310720 | tf_op jit(solution)/shard_map/all_to_all | solution.py:125
  111.5 0.0 copy-done
  111.6 17.7 %attend.2 = bf16[2560,128]{1,0:T(8,128)(2,1)} custom-call(s32[5]{0:T(128)} %rank_ref.3, s32[5]{0:T(128)} %ends_ref.3, bf16[16,3,160,128]{3,2,1,0:T(8,128)(2,1)} %copy-done, bf16[16,3,160,128]{3,2,1,0:T(8,128)(2,1)} %copy-done, bf16[16,3,160,128]{3,2,1,0:T(8,128)(2,1)} %copy-done, bf16[2560,256]{1,0:T(8,128)(2,1)} %ks_ref.3, bf16[2560,256]{1,0:T(8,128)(2,1)} %vs_ref.3), custom_call_target="tpu_custom_call" | custom-call | tf_op jit(solution)/shard_map/attend/pallas_call | solution.py:56
  129.2 0.0 all-to-all-done.3.refs_1_
  129.2 0.0 copy-start.2
  129.2 24.2 %all_to_all.20.refs_0_ = bf16[16,160,128]{2,1,0:T(8,128)(2,1)} all-to-all(bf16[16,160,128]{2,1,0:T(8,128)(2,1)} %bitcast.3), channel_id=1, replica_groups=mesh['groups'=2,'seq'=16] {'seq'}, dimensions={0} | all-to-all | bytes 1310720 | tf_op jit(solution)/shard_map/all_to_all | solution.py:125
  153.4 0.0 copy-done.2
  153.4 3.6 %unpack.1 = bf16[160,4096]{1,0:T(8,128)(2,1)} custom-call(bf16[16,160,128]{2,1,0:T(8,128)(2,1)} %all_to_all.20.refs_0_, bf16[16,160,128]{2,1,0:T(8,128)(2,1)} %copy-done.2), custom_call_target="tpu_custom_call" | custom-call | tf_op jit(solution)/shard_map/unpack/pallas_call | solution.py:103
Async XLA Ops:
  4.2 46.6 %all-to-all-start.2 = ((bf16[16,3,160,128]{3,2,1,0:T(8,128)(2,1)}), bf16[16,3,160,128]{3,2,1,0:T(8,128)(2,1)S(1)}, u32[]{:S(2)}, u32[]{:S(2)}) async-start(bf16[16,3,160,128]{3,2,1,0:T(8,128)(2,1)} %pack.3), calls=%async_computation.2 | async-start | bytes 3932160 | tf_op jit(solution)/shard_map/all_to_all | solution.py:120
  50.7 1.3 copy-start.1
  52.0 49.4 %all-to-all-start = ((bf16[16,3,160,128]{3,2,1,0:T(8,128)(2,1)}), bf16[16,3,160,128]{3,2,1,0:T(8,128)(2,1)S(1)}, u32[]{:S(2)}, u32[]{:S(2)}) async-start(bf16[16,3,160,128]{3,2,1,0:T(8,128)(2,1)} %pack.2), calls=%async_computation | async-start | bytes 3932160 | tf_op jit(solution)/shard_map/all_to_all | solution.py:120
  101.4 10.1 %copy-start = (bf16[16,3,160,128]{3,2,1,0:T(8,128)(2,1)}, bf16[16,3,160,128]{3,2,1,0:T(8,128)(2,1)S(1)}, u32[]{:S(2)}) copy-start(bf16[16,3,160,128]{3,2,1,0:T(8,128)(2,1)S(1)} %all-to-all-done.q_ref.kf_ref.vf_ref) | copy-start | bytes 5898244
  101.4 27.8 %all-to-all-start.3 = ((bf16[16,160,128]{2,1,0:T(8,128)(2,1)}), bf16[16,160,128]{2,1,0:T(8,128)(2,1)S(1)}, u32[]{:S(2)}, u32[]{:S(2)}) async-start(bf16[16,160,128]{2,1,0:T(8,128)(2,1)} %bitcast.2), calls=%async_computation.3 | async-start | bytes 1310720 | tf_op jit(solution)/shard_map/all_to_all | solution.py:125
  129.2 24.2 %copy-start.2 = (bf16[16,160,128]{2,1,0:T(8,128)(2,1)}, bf16[16,160,128]{2,1,0:T(8,128)(2,1)S(1)}, u32[]{:S(2)}) copy-start(bf16[16,160,128]{2,1,0:T(8,128)(2,1)S(1)} %all-to-all-done.3.refs_1_) | copy-start | bytes 1966084

commit v2 on v1

v2 whole, which is shorter than its diff:
```python
import functools
import math

import jax
import jax.numpy as jnp
from jax import lax
from jax.experimental import pallas as pl
from jax.experimental.pallas import tpu as pltpu
from jax.sharding import PartitionSpec as P


HEAD_DIM = 128
PATCH = 512


def attend_patch(p, rank_ref, ends_ref, query, k_ref, v_ref, ks_ref, vs_ref, out_ref, scratch):
    even, odd, top, total, mixed = scratch
    factor = math.log2(math.e) / math.sqrt(HEAD_DIM)
    mine = rank_ref[p]
    count = ends_ref[p] // PATCH
    top[...] = jnp.full(top.shape, -jnp.inf, jnp.float32)
    total[...] = jnp.zeros(total.shape, jnp.float32)
    mixed[...] = jnp.zeros(mixed.shape, jnp.float32)

    def chosen(j, new_ref, old_ref):
        at = pl.ds(pl.multiple_of(j * PATCH, PATCH), PATCH)
        return jnp.where(rank_ref[j] <= mine, new_ref[at, :], old_ref[at, :])

    def score(j):
        keys = chosen(jnp.minimum(j, count - 1), k_ref, ks_ref)
        return lax.dot_general(query, keys, (((1,), (1,)), ((), ())), preferred_element_type=jnp.float32)

    def fold(scores, j):
        before = top[...]
        higher = jnp.maximum(before, jnp.max(scores[...], axis=1, keepdims=True) * factor)
        top[...] = higher
        shrink = jnp.exp2(before - higher)
        sums = total[...] * shrink
        rounded = []
        for c in range(0, PATCH, HEAD_DIM):
            weight = jnp.exp2(scores[:, c:c + HEAD_DIM] * factor - higher)
            sums = sums + weight
            rounded.append(weight.astype(jnp.bfloat16))
        total[...] = sums
        weights = jnp.concatenate(rounded, axis=1)
        mixed[...] = mixed[...] * shrink + jnp.dot(
            weights, chosen(j, v_ref, vs_ref), preferred_element_type=jnp.float32
        )

    even[...] = score(0)

    def two(t, _):
        odd[...] = score(2 * t + 1)
        fold(even, 2 * t)

        @pl.when(2 * t + 1 < count)
        def _():
            even[...] = score(2 * t + 2)
            fold(odd, 2 * t + 1)

        return 0

    lax.fori_loop(0, (count + 1) // 2, two, 0)
    out_ref[...] = (mixed[...] / jnp.sum(total[...], axis=1, keepdims=True)).astype(jnp.bfloat16)


ATTEND_SCRATCH = [pltpu.VMEM((PATCH, PATCH), jnp.float32)] * 2 + [pltpu.VMEM((PATCH, HEAD_DIM), jnp.float32)] * 3


def attend_whole_kernel(rank_ref, ends_ref, q_ref, kf_ref, vf_ref, ks_ref, vs_ref, out_ref, *scratch):
    p = pl.program_id(0)
    flat = (q_ref.shape[0] * q_ref.shape[1], HEAD_DIM)
    query = q_ref.reshape(*flat)[pl.ds(pl.multiple_of(p * PATCH, PATCH), PATCH), :]
    keys, values = kf_ref.reshape(*flat), vf_ref.reshape(*flat)
    attend_patch(p, rank_ref, ends_ref, query, keys, values, ks_ref, vs_ref, out_ref, scratch)


def attend_whole(packed, k_stale, v_stale, rank, ends, head):
    shards_here, _, rows_here, _ = packed.shape
    total_rows = shards_here * rows_here
    part = [
        pl.BlockSpec((shards_here, None, rows_here, HEAD_DIM), lambda p, r, e, i=i: (0, i, 0, 0))
        for i in range(3)
    ]
    stale = pl.BlockSpec((total_rows, HEAD_DIM), lambda p, r, e: (0, head))
    return pl.pallas_call(
        attend_whole_kernel,
        grid_spec=pltpu.PrefetchScalarGridSpec(
            num_scalar_prefetch=2,
            grid=(rank.shape[0],),
            in_specs=[*part, stale, stale],
            out_specs=pl.BlockSpec((PATCH, HEAD_DIM), lambda p, r, e: (p, 0)),
            scratch_shapes=ATTEND_SCRATCH,
        ),
        out_shape=jax.ShapeDtypeStruct((total_rows, HEAD_DIM), jnp.bfloat16),
        name="attend_whole",
    )(rank, ends, packed, packed, packed, k_stale, v_stale)


def attend_parts_kernel(rank_ref, ends_ref, me_ref, *refs, peers):
    blocks = refs[:peers]
    ks_ref, vs_ref, out_ref, q_all, k_all, v_all, *scratch = refs[peers:]
    p = pl.program_id(0)
    rows_here = blocks[0].shape[1]

    @pl.when(p == 0)
    def _():
        for k in range(peers):
            at = pl.ds(pl.multiple_of((me_ref[0] ^ k) * rows_here, rows_here), rows_here)
            for i, ref in enumerate((q_all, k_all, v_all)):
                ref[at, :] = blocks[k][i]

    query = q_all[pl.ds(pl.multiple_of(p * PATCH, PATCH), PATCH), :]
    attend_patch(p, rank_ref, ends_ref, query, k_all, v_all, ks_ref, vs_ref, out_ref, scratch)


def attend_parts(blocks, k_stale, v_stale, rank, ends, me, head):
    peers = len(blocks)
    _, rows_here, _ = blocks[0].shape
    total_rows = peers * rows_here
    stale = pl.BlockSpec((total_rows, HEAD_DIM), lambda p, r, e, m: (0, head))
    return pl.pallas_call(
        functools.partial(attend_parts_kernel, peers=peers),
        grid_spec=pltpu.PrefetchScalarGridSpec(
            num_scalar_prefetch=3,
            grid=(rank.shape[0],),
            in_specs=[pl.BlockSpec(blocks[0].shape, lambda p, r, e, m: (0, 0, 0))] * peers + [stale, stale],
            out_specs=pl.BlockSpec((PATCH, HEAD_DIM), lambda p, r, e, m: (p, 0)),
            scratch_shapes=[pltpu.VMEM((total_rows, HEAD_DIM), jnp.bfloat16)] * 3 + ATTEND_SCRATCH,
        ),
        out_shape=jax.ShapeDtypeStruct((total_rows, HEAD_DIM), jnp.bfloat16),
        name="attend_parts",
    )(rank, ends, me, *blocks, k_stale, v_stale)


def pack_kernel(q_ref, k_ref, v_ref, out_ref, *, head, heads_here):
    for t in range(out_ref.shape[0]):
        at = (t * heads_here + head) * HEAD_DIM
        for i, ref in enumerate((q_ref, k_ref, v_ref)):
            out_ref[t, i] = ref[:, at:at + HEAD_DIM]


def pack(arrays, others, heads_here, head):
    rows_here = arrays[0].shape[0]
    each = math.gcd(others, 4)
    wide = each * heads_here * HEAD_DIM
    return pl.pallas_call(
        functools.partial(pack_kernel, head=head, heads_here=heads_here),
        grid=(others // each,),
        in_specs=[pl.BlockSpec((rows_here, wide), lambda g: (0, g))] * 3,
        out_specs=pl.BlockSpec((each, 3, rows_here, HEAD_DIM), lambda g: (g, 0, 0, 0)),
        out_shape=jax.ShapeDtypeStruct((others, 3, rows_here, HEAD_DIM), jnp.bfloat16),
        name="pack",
    )(*arrays)


def split_kernel(me_ref, q_ref, k_ref, v_ref, *outs, head, heads_here):
    for k, out_ref in enumerate(outs):
        at = pl.ds(pl.multiple_of(((me_ref[0] ^ k) * heads_here + head) * HEAD_DIM, HEAD_DIM), HEAD_DIM)
        for i, ref in enumerate((q_ref, k_ref, v_ref)):
            out_ref[i] = ref[:, at]


def split(arrays, me, peers, heads_here, head):
    rows_here = arrays[0].shape[0]
    shape = (3, rows_here, HEAD_DIM)
    return pl.pallas_call(
        functools.partial(split_kernel, head=head, heads_here=heads_here),
        grid_spec=pltpu.PrefetchScalarGridSpec(
            num_scalar_prefetch=1,
            grid=(1,),
            in_specs=[pl.BlockSpec(arrays[0].shape, lambda g, m: (0, 0))] * 3,
            out_specs=[pl.BlockSpec(shape, lambda g, m: (0, 0, 0))] * peers,
        ),
        out_shape=[jax.ShapeDtypeStruct(shape, jnp.bfloat16)] * peers,
        name="split",
    )(me, *arrays)


def unpack_kernel(*refs):
    out_ref = refs[-1]
    heads_here = len(refs) - 1
    for head in range(heads_here):
        for t in range(refs[head].shape[0]):
            at = (t * heads_here + head) * HEAD_DIM
            out_ref[:, at:at + HEAD_DIM] = refs[head][t]


def unpack(returned):
    heads_here = len(returned)
    others, rows_here, _ = returned[0].shape
    each = math.gcd(others, 4)
    return pl.pallas_call(
        unpack_kernel,
        grid=(others // each,),
        in_specs=[pl.BlockSpec((each, rows_here, HEAD_DIM), lambda g: (g, 0, 0))] * heads_here,
        out_specs=pl.BlockSpec((rows_here, each * heads_here * HEAD_DIM), lambda g: (0, g)),
        out_shape=jax.ShapeDtypeStruct((rows_here, others * heads_here * HEAD_DIM), jnp.bfloat16),
        name="unpack",
    )(*returned)


def shards(q_fresh, k_fresh, v_fresh, k_stale, v_stale, rank, ends):
    heads_here = k_stale.shape[1] // HEAD_DIM
    peers = q_fresh.shape[1] // k_stale.shape[1]
    rows_here = q_fresh.shape[0]
    fresh = (q_fresh, k_fresh, v_fresh)
    me = lax.axis_index("seq").astype(jnp.int32).reshape(1)

    def swap(array):
        return lax.all_to_all(array, "seq", split_axis=0, concat_axis=0, tiled=True)

    first = swap(pack(fresh, peers, heads_here, 0))
    later = []
    for head in range(1, heads_here):
        blocks = list(split(fresh, me, peers, heads_here, head))
        for k in (*range(1, peers // 2), *range(peers - 1, peers // 2 - 1, -1)):
            blocks[k] = lax.ppermute(blocks[k], "seq", [(s, s ^ k) for s in range(peers)])
        later.append(blocks)
    returned = []
    for head in range(heads_here):
        if head == 0:
            result = attend_whole(first, k_stale, v_stale, rank, ends, head)
        else:
            result = attend_parts(later[head - 1], k_stale, v_stale, rank, ends, me, head)
        returned.append(swap(result.reshape(peers, rows_here, HEAD_DIM)))
    return unpack(returned)


def solution(mesh):
    return jax.shard_map(
        shards,
        mesh=mesh,
        in_specs=(
            P(("groups", "seq"), None),
            P(("groups", "seq"), None),
            P(("groups", "seq"), None),
            P("groups", "seq"),
            P("groups", "seq"),
            P("groups"),
            P("groups"),
        ),
        out_specs=P(("groups", "seq"), None),
        check_vma=False,
    )
```

time: 158 us -> 163 us (1.032)
  starting transfers between devices: 27.6 us -> 46.8 us
  waiting for transfers between devices: 56.6 us -> 48.9 us
  Pallas kernels: 47.4 us -> 42.6 us
    all_to_all x3 -> x2, waiting for transfers between devices: 56.6 us -> 1.05 us  [swap(): return lax.all_to_all(array, 'seq', split_axis=0, concat_axis=0, tiled=True)]
    ppermute x0 -> x15, waiting for transfers between devices: none -> 47.9 us  [shards(): lax.ppermute(blocks[k], 'seq', [(s, s ^ k) for s in range(peers)])]
    ppermute x0 -> x15, starting transfers between devices: none -> 26.5 us  [shards(): lax.ppermute(blocks[k], 'seq', [(s, s ^ k) for s in range(peers)])]
    all_to_all x3 -> x2, starting transfers between devices: 27.6 us -> 20.3 us  [swap(): return lax.all_to_all(array, 'seq', split_axis=0, concat_axis=0, tiled=True)]
    pallas_call x2 -> x1, Pallas kernels: 8.34 us -> 4.18 us  [pack(): pl.pallas_call(functools.partial(pack_kernel, head=head, heads_here=heads...]
    pallas_call x2 -> x3, Pallas kernels: 35.4 us -> 34.8 us  [the longest x1 15.6 us: attend_parts(): pl.pallas_call(functools.partial(attend_parts_kernel, peers=peers), grid_...]
  transfers between devices with their start and end apart: 3 -> 17, of which waited for: 2 -> 8; matrix products, arithmetic and copies ran while one was open for 0% -> 0% of each run, Pallas kernels for 25% -> 21%
where the time goes in v2:
time: 163 us; the launch traced here: 162 us
  waiting for transfers between devices  48.9 us (30%)
  starting transfers between devices  46.8 us (29%)
  Pallas kernels  42.6 us (26%)
  blocking collectives  23.3 us (14%)
    ppermute x15, waiting for transfers between devices, shards(): lax.ppermute(blocks[k], 'seq', [(s, s ^ k) for s in range(peers)])  47.9 us
    ppermute x15, starting transfers between devices, shards(): lax.ppermute(blocks[k], 'seq', [(s, s ^ k) for s in range(peers)])  26.5 us
    all_to_all x1, blocking collectives, swap(): return lax.all_to_all(array, 'seq', split_axis=0, concat_axis=0, tiled=True)  23.3 us
    all_to_all x2, starting transfers between devices, swap(): return lax.all_to_all(array, 'seq', split_axis=0, concat_axis=0, tiled=True)  20.3 us
    pallas_call x1, Pallas kernels, attend_parts(): pl.pallas_call(functools.partial(attend_parts_kernel, peers=peers), grid_...  15.6 us
    pallas_call x1, Pallas kernels, attend_whole(): pl.pallas_call(attend_whole_kernel, grid_spec=pltpu.PrefetchScalarGridSpe...  15.3 us
    pallas_call x1, Pallas kernels, pack(): pl.pallas_call(functools.partial(pack_kernel, head=head, heads_here=heads...  4.18 us
    pallas_call x1, Pallas kernels, split(): pl.pallas_call(functools.partial(split_kernel, head=head, heads_here=head...  3.86 us
  transfers between devices with their start and end apart: 17, of which 8 were waited for; matrix products, arithmetic and copies ran while one was open for 0% of the time, Pallas kernels for 21%

profile of v2, /device:TPU:1, one launch (start us, length us, event | category | flops | bytes accessed | tf_op | source)
XLA Modules:
  0.0 162.4 jit_solution(5827845100513087980)
XLA Ops:
  0.0 4.2 %pack.1 = bf16[16,3,160,128]{3,2,1,0:T(8,128)(2,1)} custom-call(bf16[160,4096]{1,0:T(8,128)(2,1)} %q_ref.3, bf16[160,4096]{1,0:T(8,128)(2,1)} %k_ref.3, bf16[160,4096]{1,0:T(8,128)(2,1)} %v_ref.3), custom_call_target="tpu_custom_call" | custom-call | tf_op jit(solution)/shard_map/pack/pallas_call | solution.py:147
  4.2 7.3 %all-to-all-start = ((bf16[16,3,160,128]{3,2,1,0:T(8,128)(2,1)}), bf16[16,3,160,128]{3,2,1,0:T(8,128)(2,1)S(1)}, u32[]{:S(2)}, u32[]{:S(2)}) async-start(bf16[16,3,160,128]{3,2,1,0:T(8,128)(2,1)} %pack.1), calls=%async_computation | async-start | bytes 3932160 | tf_op jit(solution)/shard_map/all_to_all | solution.py:211
  11.5 3.9 %split.1 = (bf16[3,160,128]{2,1,0:T(8,128)(2,1)}, bf16[3,160,128]{2,1,0:T(8,128)(2,1)}, bf16[3,160,128]{2,1,0:T(8,128)(2,1)}, bf16[3,160,128]{2,1,0:T(8,128)(2,1...) custom-call(s32[1]{0:T(128)} %bitcast.1.me_ref, ...), custom_call_target="tpu_custom_call" | custom-call | tf_op jit(solution)/shard_map/split/pallas_call | solution.py:167
  15.4 0.1 collective-permute-start
  15.5 1.6 %collective-permute-start.1 = (bf16[3,160,128]{2,1,0:T(8,128)(2,1)}, bf16[3,160,128]{2,1,0:T(8,128)(2,1)S(1)}, u32[]{:S(2)}, u32[]{:S(2)}) collective-permute-start(bf16[3,160,128]{2,1,0:T(8,128)(2,1)} %get-tuple-element.23), channel_id=1, source_target_pairs={{0,2},{1,3},{2,0},{3,1},{4,6},{5,7},{6,4},{7,5},{8,10},{9,11},{10,... | collective-permute-start | bytes 368648 | tf_op jit(solution)/shard_map/ppermute | solution.py:218
  17.1 0.4 collective-permute-start.2
  17.5 1.4 collective-permute-start.3
  18.9 0.3 collective-permute-start.4
  19.2 0.0 collective-permute-done.refs_1_
  19.2 2.4 %collective-permute-start.5 = (bf16[3,160,128]{2,1,0:T(8,128)(2,1)}, bf16[3,160,128]{2,1,0:T(8,128)(2,1)S(1)}, u32[]{:S(2)}, u32[]{:S(2)}) collective-permute-start(bf16[3,160,128]{2,1,0:T(8,128)(2,1)} %get-tuple-element.27), channel_id=1, source_target_pairs={{0,6},{1,7},{2,4},{3,5},{4,2},{5,3},{6,0},{7,1},{8,14},{9,15},{10,... | collective-permute-start | bytes 368648 | tf_op jit(solution)/shard_map/ppermute | solution.py:218
  21.5 6.4 %collective-permute-done.1.refs_2_ = bf16[3,160,128]{2,1,0:T(8,128)(2,1)S(1)} collective-permute-done((bf16[3,160,128]{2,1,0:T(8,128)(2,1)}, bf16[3,160,128]{2,1,0:T(8,128)(2,1)S(1)}, u32[]{:S(2)}, u32[]{:S(2)}) %collective-permute-start.1) | collective-permute-done | bytes 122912 | tf_op jit(solution)/shard_map/ppermute | solution.py:218
  28.0 1.6 collective-permute-start.6
  29.5 5.3 %collective-permute-done.2.refs_3_ = bf16[3,160,128]{2,1,0:T(8,128)(2,1)S(1)} collective-permute-done((bf16[3,160,128]{2,1,0:T(8,128)(2,1)}, bf16[3,160,128]{2,1,0:T(8,128)(2,1)S(1)}, u32[]{:S(2)}, u32[]{:S(2)}) %collective-permute-start.2) | collective-permute-done | bytes 122912 | tf_op jit(solution)/shard_map/ppermute | solution.py:218
  34.8 0.0 collective-permute-start.7
  34.8 11.8 %collective-permute-done.3.refs_4_ = bf16[3,160,128]{2,1,0:T(8,128)(2,1)S(1)} collective-permute-done((bf16[3,160,128]{2,1,0:T(8,128)(2,1)}, bf16[3,160,128]{2,1,0:T(8,128)(2,1)S(1)}, u32[]{:S(2)}, u32[]{:S(2)}) %collective-permute-start.3) | collective-permute-done | bytes 122912 | tf_op jit(solution)/shard_map/ppermute | solution.py:218
  46.6 5.0 %collective-permute-start.8 = (bf16[3,160,128]{2,1,0:T(8,128)(2,1)}, bf16[3,160,128]{2,1,0:T(8,128)(2,1)S(1)}, u32[]{:S(2)}, u32[]{:S(2)}) collective-permute-start(bf16[3,160,128]{2,1,0:T(8,128)(2,1)} %get-tuple-element.30), channel_id=1, source_target_pairs={{0,9},{1,8},{2,11},{3,10},{4,13},{5,12},{6,15},{7,14},{8,1},{9,0},... | collective-permute-start | bytes 368648 | tf_op jit(solution)/shard_map/ppermute | solution.py:218
  51.7 0.0 collective-permute-done.4.refs_5_
  51.7 3.4 %collective-permute-start.9 = (bf16[3,160,128]{2,1,0:T(8,128)(2,1)}, bf16[3,160,128]{2,1,0:T(8,128)(2,1)S(1)}, u32[]{:S(2)}, u32[]{:S(2)}) collective-permute-start(bf16[3,160,128]{2,1,0:T(8,128)(2,1)} %get-tuple-element.31), channel_id=1, source_target_pairs={{0,10},{1,11},{2,8},{3,9},{4,14},{5,15},{6,12},{7,13},{8,2},{9,3},... | collective-permute-start | bytes 368648 | tf_op jit(solution)/shard_map/ppermute | solution.py:218
  55.1 0.0 collective-permute-done.5.refs_6_
  55.1 2.8 %collective-permute-start.10 = (bf16[3,160,128]{2,1,0:T(8,128)(2,1)}, bf16[3,160,128]{2,1,0:T(8,128)(2,1)S(1)}, u32[]{:S(2)}, u32[]{:S(2)}) collective-permute-start(bf16[3,160,128]{2,1,0:T(8,128)(2,1)} %get-tuple-element.32), channel_id=1, source_target_pairs={{0,11},{1,10},{2,9},{3,8},{4,15},{5,14},{6,13},{7,12},{8,3},{9,2},... | collective-permute-start | bytes 368648 | tf_op jit(solution)/shard_map/ppermute | solution.py:218
  57.8 0.0 collective-permute-done.6.refs_7_
  57.9 1.3 collective-permute-start.11
  59.2 14.4 %collective-permute-done.7.refs_8_ = bf16[3,160,128]{2,1,0:T(8,128)(2,1)S(1)} collective-permute-done((bf16[3,160,128]{2,1,0:T(8,128)(2,1)}, bf16[3,160,128]{2,1,0:T(8,128)(2,1)S(1)}, u32[]{:S(2)}, u32[]{:S(2)}) %collective-permute-start.7) | collective-permute-done | bytes 122912 | tf_op jit(solution)/shard_map/ppermute | solution.py:218
  73.6 1.8 %collective-permute-start.12 = (bf16[3,160,128]{2,1,0:T(8,128)(2,1)}, bf16[3,160,128]{2,1,0:T(8,128)(2,1)}, u32[]{:S(2)}, u32[]{:S(2)}) collective-permute-start(bf16[3,160,128]{2,1,0:T(8,128)(2,1)} %get-tuple-element.34), channel_id=1, source_target_pairs={{0,13},{1,12},{2,15},{3,14},{4,9},{5,8},{6,11},{7,10},{8,5},{9,4},... | collective-permute-start | bytes 368648 | tf_op jit(solution)/shard_map/ppermute | solution.py:218
  75.4 1.6 %collective-permute-done.8.refs_9_ = bf16[3,160,128]{2,1,0:T(8,128)(2,1)S(1)} collective-permute-done((bf16[3,160,128]{2,1,0:T(8,128)(2,1)}, bf16[3,160,128]{2,1,0:T(8,128)(2,1)S(1)}, u32[]{:S(2)}, u32[]{:S(2)}) %collective-permute-start.8) | collective-permute-done | bytes 122912 | tf_op jit(solution)/shard_map/ppermute | solution.py:218
  77.0 2.6 %collective-permute-start.13 = (bf16[3,160,128]{2,1,0:T(8,128)(2,1)}, bf16[3,160,128]{2,1,0:T(8,128)(2,1)}, u32[]{:S(2)}, u32[]{:S(2)}) collective-permute-start(bf16[3,160,128]{2,1,0:T(8,128)(2,1)} %get-tuple-element.35), channel_id=1, source_target_pairs={{0,14},{1,15},{2,12},{3,13},{4,10},{5,11},{6,8},{7,9},{8,6},{9,7},... | collective-permute-start | bytes 368648 | tf_op jit(solution)/shard_map/ppermute | solution.py:218
  79.6 2.7 %collective-permute-done.9.refs_10_ = bf16[3,160,128]{2,1,0:T(8,128)(2,1)S(1)} collective-permute-done((bf16[3,160,128]{2,1,0:T(8,128)(2,1)}, bf16[3,160,128]{2,1,0:T(8,128)(2,1)S(1)}, u32[]{:S(2)}, u32[]{:S(2)}) %collective-permute-start.9) | collective-permute-done | bytes 122912 | tf_op jit(solution)/shard_map/ppermute | solution.py:218
  82.3 1.9 %collective-permute-start.14 = (bf16[3,160,128]{2,1,0:T(8,128)(2,1)}, bf16[3,160,128]{2,1,0:T(8,128)(2,1)}, u32[]{:S(2)}, u32[]{:S(2)}) collective-permute-start(bf16[3,160,128]{2,1,0:T(8,128)(2,1)} %get-tuple-element.36), channel_id=1, source_target_pairs={{0,15},{1,14},{2,13},{3,12},{4,11},{5,10},{6,9},{7,8},{8,7},{9,6},... | collective-permute-start | bytes 368648 | tf_op jit(solution)/shard_map/ppermute | solution.py:218
  84.2 5.6 %collective-permute-done.10.refs_11_ = bf16[3,160,128]{2,1,0:T(8,128)(2,1)S(1)} collective-permute-done((bf16[3,160,128]{2,1,0:T(8,128)(2,1)}, bf16[3,160,128]{2,1,0:T(8,128)(2,1)S(1)}, u32[]{:S(2)}, u32[]{:S(2)}) %collective-permute-start.10) | collective-permute-done | bytes 122912 | tf_op jit(solution)/shard_map/ppermute | solution.py:218
  89.8 0.0 collective-permute-done.11.refs_12_
  89.8 0.0 collective-permute-done.12.refs_13_
  89.8 0.0 collective-permute-done.13.refs_14_
  89.8 0.0 collective-permute-done.14.refs_15_
  89.8 0.0 copy-done.2
  89.8 0.0 copy-done.3
  89.8 0.0 copy-done.4
  89.8 0.0 copy-done.5
  89.8 0.0 copy-done.6
  89.9 0.5 copy-done.12
  90.4 0.1 copy-done.13
  90.5 15.6 %attend_parts.1 = bf16[2560,128]{1,0:T(8,128)(2,1)} custom-call(s32[5]{0:T(128)} %rank_ref.3, s32[5]{0:T(128)} %ends_ref.3, s32[1]{0:T(128)} %bitcast.1.me_ref, bf16[3,160,128]{2,1,0:T(8,128)(2,1)} %get-tuple-element.21.refs_0_, bf16[3,160,128]{2,1,0:T(8,128)(2,1)} %copy-done.2, bf16[3,160,128]{2,1,0:T(8,128)(2,1)} %copy-done.3, ...), custom_call_target="tpu_custom_call" | custom-call | tf_op jit(solution)/shard_map/attend_parts/pallas_call | solution.py:122
  106.1 0.0 all-to-all-done.q_ref.kf_ref.vf_ref
  106.1 0.0 copy-start
  106.1 13.0 %all-to-all-start.2 = ((bf16[16,160,128]{2,1,0:T(8,128)(2,1)}), bf16[16,160,128]{2,1,0:T(8,128)(2,1)S(1)}, u32[]{:S(2)}, u32[]{:S(2)}) async-start(bf16[16,160,128]{2,1,0:T(8,128)(2,1)} %bitcast.4), calls=%async_computation.2 | async-start | bytes 1310720 | tf_op jit(solution)/shard_map/all_to_all | solution.py:211
  119.1 15.3 %attend_whole.1 = bf16[2560,128]{1,0:T(8,128)(2,1)} custom-call(s32[5]{0:T(128)} %rank_ref.3, s32[5]{0:T(128)} %ends_ref.3, bf16[16,3,160,128]{3,2,1,0:T(8,128)(2,1)} %copy-done, bf16[16,3,160,128]{3,2,1,0:T(8,128)(2,1)} %copy-done, bf16[16,3,160,128]{3,2,1,0:T(8,128)(2,1)} %copy-done, bf16[2560,256]{1,0:T(8,128)(2,1)} %refs_16_.1, bf16[2560,256]{1,0:T(8,128)(2,1)} %refs_17_.1), custom_call_target="tpu_custom_call" | custom-call | tf_op jit(solution)/shard_map/attend_whole/pallas_call | solution.py:86
  134.4 1.0 all-to-all-done.2.refs_1_
  135.5 23.3 %all_to_all.15.refs_0_ = bf16[16,160,128]{2,1,0:T(8,128)(2,1)} all-to-all(bf16[16,160,128]{2,1,0:T(8,128)(2,1)} %bitcast.3), channel_id=1, replica_groups=mesh['groups'=2,'seq'=16] {'seq'}, dimensions={0} | all-to-all | bytes 1310720 | tf_op jit(solution)/shard_map/all_to_all | solution.py:211
  158.8 3.6 %unpack.1 = bf16[160,4096]{1,0:T(8,128)(2,1)} custom-call(bf16[16,160,128]{2,1,0:T(8,128)(2,1)} %all_to_all.15.refs_0_, bf16[16,160,128]{2,1,0:T(8,128)(2,1)} %copy-done.1), custom_call_target="tpu_custom_call" | custom-call | tf_op jit(solution)/shard_map/unpack/pallas_call | solution.py:193
  (20 shorter events, 0.0 us)
Async XLA Ops:
  4.2 101.9 %all-to-all-start = ((bf16[16,3,160,128]{3,2,1,0:T(8,128)(2,1)}), bf16[16,3,160,128]{3,2,1,0:T(8,128)(2,1)S(1)}, u32[]{:S(2)}, u32[]{:S(2)}) async-start(bf16[16,3,160,128]{3,2,1,0:T(8,128)(2,1)} %pack.1), calls=%async_computation | async-start | bytes 3932160 | tf_op jit(solution)/shard_map/all_to_all | solution.py:211
  15.4 3.8 %collective-permute-start = (bf16[3,160,128]{2,1,0:T(8,128)(2,1)}, bf16[3,160,128]{2,1,0:T(8,128)(2,1)S(1)}, u32[]{:S(2)}, u32[]{:S(2)}) collective-permute-start(bf16[3,160,128]{2,1,0:T(8,128)(2,1)} %get-tuple-element.22), channel_id=1, source_target_pairs={{0,1},{1,0},{2,3},{3,2},{4,5},{5,4},{6,7},{7,6},{8,9},{9,8},{10,11... | collective-permute-start | bytes 368648 | tf_op jit(solution)/shard_map/ppermute | solution.py:218
  15.5 12.5 %collective-permute-start.1 = (bf16[3,160,128]{2,1,0:T(8,128)(2,1)}, bf16[3,160,128]{2,1,0:T(8,128)(2,1)S(1)}, u32[]{:S(2)}, u32[]{:S(2)}) collective-permute-start(bf16[3,160,128]{2,1,0:T(8,128)(2,1)} %get-tuple-element.23), channel_id=1, source_target_pairs={{0,2},{1,3},{2,0},{3,1},{4,6},{5,7},{6,4},{7,5},{8,10},{9,11},{10,... | collective-permute-start | bytes 368648 | tf_op jit(solution)/shard_map/ppermute | solution.py:218
  17.1 17.7 %collective-permute-start.2 = (bf16[3,160,128]{2,1,0:T(8,128)(2,1)}, bf16[3,160,128]{2,1,0:T(8,128)(2,1)S(1)}, u32[]{:S(2)}, u32[]{:S(2)}) collective-permute-start(bf16[3,160,128]{2,1,0:T(8,128)(2,1)} %get-tuple-element.24), channel_id=1, source_target_pairs={{0,3},{1,2},{2,1},{3,0},{4,7},{5,6},{6,5},{7,4},{8,11},{9,10},{10,... | collective-permute-start | bytes 368648 | tf_op jit(solution)/shard_map/ppermute | solution.py:218
  17.5 29.1 %collective-permute-start.3 = (bf16[3,160,128]{2,1,0:T(8,128)(2,1)}, bf16[3,160,128]{2,1,0:T(8,128)(2,1)S(1)}, u32[]{:S(2)}, u32[]{:S(2)}) collective-permute-start(bf16[3,160,128]{2,1,0:T(8,128)(2,1)} %get-tuple-element.25), channel_id=1, source_target_pairs={{0,4},{1,5},{2,6},{3,7},{4,0},{5,1},{6,2},{7,3},{8,12},{9,13},{10,... | collective-permute-start | bytes 368648 | tf_op jit(solution)/shard_map/ppermute | solution.py:218
  18.9 32.8 %collective-permute-start.4 = (bf16[3,160,128]{2,1,0:T(8,128)(2,1)}, bf16[3,160,128]{2,1,0:T(8,128)(2,1)S(1)}, u32[]{:S(2)}, u32[]{:S(2)}) collective-permute-start(bf16[3,160,128]{2,1,0:T(8,128)(2,1)} %get-tuple-element.26), channel_id=1, source_target_pairs={{0,5},{1,4},{2,7},{3,6},{4,1},{5,0},{6,3},{7,2},{8,13},{9,12},{10,... | collective-permute-start | bytes 368648 | tf_op jit(solution)/shard_map/ppermute | solution.py:218
  19.2 70.6 %copy-start.2 = (bf16[3,160,128]{2,1,0:T(8,128)(2,1)}, bf16[3,160,128]{2,1,0:T(8,128)(2,1)S(1)}, u32[]{:S(2)}) copy-start(bf16[3,160,128]{2,1,0:T(8,128)(2,1)S(1)} %collective-permute-done.refs_1_) | copy-start | bytes 368644
  19.2 35.9 %collective-permute-start.5 = (bf16[3,160,128]{2,1,0:T(8,128)(2,1)}, bf16[3,160,128]{2,1,0:T(8,128)(2,1)S(1)}, u32[]{:S(2)}, u32[]{:S(2)}) collective-permute-start(bf16[3,160,128]{2,1,0:T(8,128)(2,1)} %get-tuple-element.27), channel_id=1, source_target_pairs={{0,6},{1,7},{2,4},{3,5},{4,2},{5,3},{6,0},{7,1},{8,14},{9,15},{10,... | collective-permute-start | bytes 368648 | tf_op jit(solution)/shard_map/ppermute | solution.py:218
  28.0 61.8 %copy-start.3 = (bf16[3,160,128]{2,1,0:T(8,128)(2,1)}, bf16[3,160,128]{2,1,0:T(8,128)(2,1)S(1)}, u32[]{:S(2)}) copy-start(bf16[3,160,128]{2,1,0:T(8,128)(2,1)S(1)} %collective-permute-done.1.refs_2_) | copy-start | bytes 368644
  28.0 29.9 %collective-permute-start.6 = (bf16[3,160,128]{2,1,0:T(8,128)(2,1)}, bf16[3,160,128]{2,1,0:T(8,128)(2,1)S(1)}, u32[]{:S(2)}, u32[]{:S(2)}) collective-permute-start(bf16[3,160,128]{2,1,0:T(8,128)(2,1)} %get-tuple-element.28), channel_id=1, source_target_pairs={{0,7},{1,6},{2,5},{3,4},{4,3},{5,2},{6,1},{7,0},{8,15},{9,14},{10,... | collective-permute-start | bytes 368648 | tf_op jit(solution)/shard_map/ppermute | solution.py:218
  34.8 55.0 %copy-start.4 = (bf16[3,160,128]{2,1,0:T(8,128)(2,1)}, bf16[3,160,128]{2,1,0:T(8,128)(2,1)S(1)}, u32[]{:S(2)}) copy-start(bf16[3,160,128]{2,1,0:T(8,128)(2,1)S(1)} %collective-permute-done.2.refs_3_) | copy-start | bytes 368644
  34.8 38.7 %collective-permute-start.7 = (bf16[3,160,128]{2,1,0:T(8,128)(2,1)}, bf16[3,160,128]{2,1,0:T(8,128)(2,1)S(1)}, u32[]{:S(2)}, u32[]{:S(2)}) collective-permute-start(bf16[3,160,128]{2,1,0:T(8,128)(2,1)} %get-tuple-element.29), channel_id=1, source_target_pairs={{0,8},{1,9},{2,10},{3,11},{4,12},{5,13},{6,14},{7,15},{8,0},{9,1},... | collective-permute-start | bytes 368648 | tf_op jit(solution)/shard_map/ppermute | solution.py:218
  46.6 43.2 %copy-start.5 = (bf16[3,160,128]{2,1,0:T(8,128)(2,1)}, bf16[3,160,128]{2,1,0:T(8,128)(2,1)S(1)}, u32[]{:S(2)}) copy-start(bf16[3,160,128]{2,1,0:T(8,128)(2,1)S(1)} %collective-permute-done.3.refs_4_) | copy-start | bytes 368644
  46.6 30.4 %collective-permute-start.8 = (bf16[3,160,128]{2,1,0:T(8,128)(2,1)}, bf16[3,160,128]{2,1,0:T(8,128)(2,1)S(1)}, u32[]{:S(2)}, u32[]{:S(2)}) collective-permute-start(bf16[3,160,128]{2,1,0:T(8,128)(2,1)} %get-tuple-element.30), channel_id=1, source_target_pairs={{0,9},{1,8},{2,11},{3,10},{4,13},{5,12},{6,15},{7,14},{8,1},{9,0},... | collective-permute-start | bytes 368648 | tf_op jit(solution)/shard_map/ppermute | solution.py:218
  51.7 38.1 %copy-start.6 = (bf16[3,160,128]{2,1,0:T(8,128)(2,1)}, bf16[3,160,128]{2,1,0:T(8,128)(2,1)S(1)}, u32[]{:S(2)}) copy-start(bf16[3,160,128]{2,1,0:T(8,128)(2,1)S(1)} %collective-permute-done.4.refs_5_) | copy-start | bytes 368644
  51.7 30.6 %collective-permute-start.9 = (bf16[3,160,128]{2,1,0:T(8,128)(2,1)}, bf16[3,160,128]{2,1,0:T(8,128)(2,1)S(1)}, u32[]{:S(2)}, u32[]{:S(2)}) collective-permute-start(bf16[3,160,128]{2,1,0:T(8,128)(2,1)} %get-tuple-element.31), channel_id=1, source_target_pairs={{0,10},{1,11},{2,8},{3,9},{4,14},{5,15},{6,12},{7,13},{8,2},{9,3},... | collective-permute-start | bytes 368648 | tf_op jit(solution)/shard_map/ppermute | solution.py:218
  55.1 34.8 %copy-start.7 = (bf16[3,160,128]{2,1,0:T(8,128)(2,1)}, bf16[3,160,128]{2,1,0:T(8,128)(2,1)S(1)}, u32[]{:S(2)}) copy-start(bf16[3,160,128]{2,1,0:T(8,128)(2,1)S(1)} %collective-permute-done.5.refs_6_) | copy-start | bytes 368644
  55.1 34.7 %collective-permute-start.10 = (bf16[3,160,128]{2,1,0:T(8,128)(2,1)}, bf16[3,160,128]{2,1,0:T(8,128)(2,1)S(1)}, u32[]{:S(2)}, u32[]{:S(2)}) collective-permute-start(bf16[3,160,128]{2,1,0:T(8,128)(2,1)} %get-tuple-element.32), channel_id=1, source_target_pairs={{0,11},{1,10},{2,9},{3,8},{4,15},{5,14},{6,13},{7,12},{8,3},{9,2},... | collective-permute-start | bytes 368648 | tf_op jit(solution)/shard_map/ppermute | solution.py:218
  57.8 32.0 %copy-start.8 = (bf16[3,160,128]{2,1,0:T(8,128)(2,1)}, bf16[3,160,128]{2,1,0:T(8,128)(2,1)S(1)}, u32[]{:S(2)}) copy-start(bf16[3,160,128]{2,1,0:T(8,128)(2,1)S(1)} %collective-permute-done.6.refs_7_) | copy-start | bytes 368644
  57.9 31.9 %collective-permute-start.11 = (bf16[3,160,128]{2,1,0:T(8,128)(2,1)}, bf16[3,160,128]{2,1,0:T(8,128)(2,1)S(1)}, u32[]{:S(2)}, u32[]{:S(2)}) collective-permute-start(bf16[3,160,128]{2,1,0:T(8,128)(2,1)} %get-tuple-element.33), channel_id=1, source_target_pairs={{0,12},{1,13},{2,14},{3,15},{4,8},{5,9},{6,10},{7,11},{8,4},{9,5},... | collective-permute-start | bytes 368648 | tf_op jit(solution)/shard_map/ppermute | solution.py:218
  73.6 16.3 %copy-start.9 = (bf16[3,160,128]{2,1,0:T(8,128)(2,1)}, bf16[3,160,128]{2,1,0:T(8,128)(2,1)S(1)}, u32[]{:S(2)}) copy-start(bf16[3,160,128]{2,1,0:T(8,128)(2,1)S(1)} %collective-permute-done.7.refs_8_) | copy-start | bytes 368644
  73.6 16.2 %collective-permute-start.12 = (bf16[3,160,128]{2,1,0:T(8,128)(2,1)}, bf16[3,160,128]{2,1,0:T(8,128)(2,1)}, u32[]{:S(2)}, u32[]{:S(2)}) collective-permute-start(bf16[3,160,128]{2,1,0:T(8,128)(2,1)} %get-tuple-element.34), channel_id=1, source_target_pairs={{0,13},{1,12},{2,15},{3,14},{4,9},{5,8},{6,11},{7,10},{8,5},{9,4},... | collective-permute-start | bytes 368648 | tf_op jit(solution)/shard_map/ppermute | solution.py:218
  77.0 12.8 %copy-start.10 = (bf16[3,160,128]{2,1,0:T(8,128)(2,1)}, bf16[3,160,128]{2,1,0:T(8,128)(2,1)S(1)}, u32[]{:S(2)}) copy-start(bf16[3,160,128]{2,1,0:T(8,128)(2,1)S(1)} %collective-permute-done.8.refs_9_) | copy-start | bytes 368644
  77.0 12.7 %collective-permute-start.13 = (bf16[3,160,128]{2,1,0:T(8,128)(2,1)}, bf16[3,160,128]{2,1,0:T(8,128)(2,1)}, u32[]{:S(2)}, u32[]{:S(2)}) collective-permute-start(bf16[3,160,128]{2,1,0:T(8,128)(2,1)} %get-tuple-element.35), channel_id=1, source_target_pairs={{0,14},{1,15},{2,12},{3,13},{4,10},{5,11},{6,8},{7,9},{8,6},{9,7},... | collective-permute-start | bytes 368648 | tf_op jit(solution)/shard_map/ppermute | solution.py:218
  82.3 7.6 %copy-start.11 = (bf16[3,160,128]{2,1,0:T(8,128)(2,1)}, bf16[3,160,128]{2,1,0:T(8,128)(2,1)S(1)}, u32[]{:S(2)}) copy-start(bf16[3,160,128]{2,1,0:T(8,128)(2,1)S(1)} %collective-permute-done.9.refs_10_) | copy-start | bytes 368644
  82.3 7.5 %collective-permute-start.14 = (bf16[3,160,128]{2,1,0:T(8,128)(2,1)}, bf16[3,160,128]{2,1,0:T(8,128)(2,1)}, u32[]{:S(2)}, u32[]{:S(2)}) collective-permute-start(bf16[3,160,128]{2,1,0:T(8,128)(2,1)} %get-tuple-element.36), channel_id=1, source_target_pairs={{0,15},{1,14},{2,13},{3,12},{4,11},{5,10},{6,9},{7,8},{8,7},{9,6},... | collective-permute-start | bytes 368648 | tf_op jit(solution)/shard_map/ppermute | solution.py:218
  89.8 0.7 copy-start.12
  89.8 0.7 copy-start.13
  106.1 13.0 %copy-start = (bf16[16,3,160,128]{3,2,1,0:T(8,128)(2,1)}, bf16[16,3,160,128]{3,2,1,0:T(8,128)(2,1)S(1)}, u32[]{:S(2)}) copy-start(bf16[16,3,160,128]{3,2,1,0:T(8,128)(2,1)S(1)} %all-to-all-done.q_ref.kf_ref.vf_ref) | copy-start | bytes 5898244
  106.1 29.3 %all-to-all-start.2 = ((bf16[16,160,128]{2,1,0:T(8,128)(2,1)}), bf16[16,160,128]{2,1,0:T(8,128)(2,1)S(1)}, u32[]{:S(2)}, u32[]{:S(2)}) async-start(bf16[16,160,128]{2,1,0:T(8,128)(2,1)} %bitcast.4), calls=%async_computation.2 | async-start | bytes 1310720 | tf_op jit(solution)/shard_map/all_to_all | solution.py:211
  135.5 23.3 %copy-start.1 = (bf16[16,160,128]{2,1,0:T(8,128)(2,1)}, bf16[16,160,128]{2,1,0:T(8,128)(2,1)S(1)}, u32[]{:S(2)}) copy-start(bf16[16,160,128]{2,1,0:T(8,128)(2,1)S(1)} %all-to-all-done.2.refs_1_) | copy-start | bytes 1966084

commit v3 on v2

--- a/solution.py
+++ b/solution.py
@@ -133,23 +133,38 @@
     )(rank, ends, me, *blocks, k_stale, v_stale)
 
 
-def pack_kernel(q_ref, k_ref, v_ref, out_ref, *, head, heads_here):
+def pack_kernel(q_ref, k_ref, v_ref, out_ref, held, read_sem, write_sem, *, head, heads_here):
+    reads, writes = [], []
     for t in range(out_ref.shape[0]):
         at = (t * heads_here + head) * HEAD_DIM
-        for i, ref in enumerate((q_ref, k_ref, v_ref)):
-            out_ref[t, i] = ref[:, at:at + HEAD_DIM]
+        reads.append([
+            pltpu.make_async_copy(ref.at[:, at:at + HEAD_DIM], held.at[t, i], read_sem.at[t, i])
+            for i, ref in enumerate((q_ref, k_ref, v_ref))
+        ])
+        for copy in reads[t]:
+            copy.start()
+    for t in range(out_ref.shape[0]):
+        for copy in reads[t]:
+            copy.wait()
+        writes.append(pltpu.make_async_copy(held.at[t], out_ref.at[t], write_sem.at[t]))
+        writes[t].start()
+    for copy in writes:
+        copy.wait()
 
 
 def pack(arrays, others, heads_here, head):
     rows_here = arrays[0].shape[0]
-    each = math.gcd(others, 4)
-    wide = each * heads_here * HEAD_DIM
+    shape = (others, 3, rows_here, HEAD_DIM)
     return pl.pallas_call(
         functools.partial(pack_kernel, head=head, heads_here=heads_here),
-        grid=(others // each,),
-        in_specs=[pl.BlockSpec((rows_here, wide), lambda g: (0, g))] * 3,
-        out_specs=pl.BlockSpec((each, 3, rows_here, HEAD_DIM), lambda g: (g, 0, 0, 0)),
-        out_shape=jax.ShapeDtypeStruct((others, 3, rows_here, HEAD_DIM), jnp.bfloat16),
+        in_specs=[pl.BlockSpec(memory_space=pl.ANY)] * 3,
+        out_specs=pl.BlockSpec(memory_space=pl.ANY),
+        out_shape=jax.ShapeDtypeStruct(shape, jnp.bfloat16),
+        scratch_shapes=[
+            pltpu.VMEM(shape, jnp.bfloat16),
+            pltpu.SemaphoreType.DMA((others, 3)),
+            pltpu.SemaphoreType.DMA((others,)),
+        ],
         name="pack",
     )(*arrays)
 
@@ -189,7 +204,7 @@
 def unpack(returned):
     heads_here = len(returned)
     others, rows_here, _ = returned[0].shape
-    each = math.gcd(others, 4)
+    each = math.gcd(others, 8)
     return pl.pallas_call(
         unpack_kernel,
         grid=(others // each,),
@@ -214,7 +229,7 @@
     later = []
     for head in range(1, heads_here):
         blocks = list(split(fresh, me, peers, heads_here, head))
-        for k in (*range(1, peers // 2), *range(peers - 1, peers // 2 - 1, -1)):
+        for k in range(1, peers):
             blocks[k] = lax.ppermute(blocks[k], "seq", [(s, s ^ k) for s in range(peers)])
         later.append(blocks)
     returned = []

time: 163 us -> 161 us (0.988)
  Pallas kernels: 42.6 us -> 39.9 us
  transfers between devices with their start and end apart: 17 -> 17, of which waited for: 8 -> 8; matrix products, arithmetic and copies ran while one was open for 0% -> 0% of each run, Pallas kernels for 21% -> 22%
where the time goes in v3:
time: 161 us; the launch traced here: 160 us
  waiting for transfers between devices  48.9 us (30%)
  starting transfers between devices  46.9 us (29%)
  Pallas kernels  39.9 us (25%)
  blocking collectives  23.3 us (14%)
    ppermute x15, waiting for transfers between devices, shards(): lax.ppermute(blocks[k], 'seq', [(s, s ^ k) for s in range(peers)])  47.9 us
    ppermute x15, starting transfers between devices, shards(): lax.ppermute(blocks[k], 'seq', [(s, s ^ k) for s in range(peers)])  26.5 us
    all_to_all x1, blocking collectives, swap(): return lax.all_to_all(array, 'seq', split_axis=0, concat_axis=0, tiled=True)  23.3 us
    all_to_all x2, starting transfers between devices, swap(): return lax.all_to_all(array, 'seq', split_axis=0, concat_axis=0, tiled=True)  20.4 us
    pallas_call x1, Pallas kernels, attend_parts(): pl.pallas_call(functools.partial(attend_parts_kernel, peers=peers), grid_...  15.6 us
    pallas_call x1, Pallas kernels, attend_whole(): pl.pallas_call(attend_whole_kernel, grid_spec=pltpu.PrefetchScalarGridSpe...  15.3 us
    pallas_call x1, Pallas kernels, split(): pl.pallas_call(functools.partial(split_kernel, head=head, heads_here=head...  3.86 us
  transfers between devices with their start and end apart: 17, of which 8 were waited for; matrix products, arithmetic and copies ran while one was open for 0% of the time, Pallas kernels for 22%

profile of v3, /device:TPU:1, one launch (start us, length us, event | category | flops | bytes accessed | tf_op | source)
XLA Modules:
  0.0 159.7 jit_solution(15289669364293608304)
XLA Ops:
  0.0 2.8 %pack.1 = bf16[16,3,160,128]{3,2,1,0:T(8,128)(2,1)} custom-call(bf16[160,4096]{1,0:T(8,128)(2,1)} %q_ref.3, bf16[160,4096]{1,0:T(8,128)(2,1)} %k_ref.3, bf16[160,4096]{1,0:T(8,128)(2,1)} %v_ref.3), custom_call_target="tpu_custom_call" | custom-call | tf_op jit(solution)/shard_map/pack/pallas_call | solution.py:158
  2.8 7.4 %all-to-all-start = ((bf16[16,3,160,128]{3,2,1,0:T(8,128)(2,1)}), bf16[16,3,160,128]{3,2,1,0:T(8,128)(2,1)S(1)}, u32[]{:S(2)}, u32[]{:S(2)}) async-start(bf16[16,3,160,128]{3,2,1,0:T(8,128)(2,1)} %pack.1), calls=%async_computation | async-start | bytes 3932160 | tf_op jit(solution)/shard_map/all_to_all | solution.py:226
  10.1 3.9 %split.1 = (bf16[3,160,128]{2,1,0:T(8,128)(2,1)}, bf16[3,160,128]{2,1,0:T(8,128)(2,1)}, bf16[3,160,128]{2,1,0:T(8,128)(2,1)}, bf16[3,160,128]{2,1,0:T(8,128)(2,1...) custom-call(s32[1]{0:T(128)} %bitcast.1.me_ref, ...), custom_call_target="tpu_custom_call" | custom-call | tf_op jit(solution)/shard_map/split/pallas_call | solution.py:182
  14.0 0.1 collective-permute-start
  14.1 1.6 %collective-permute-start.1 = (bf16[3,160,128]{2,1,0:T(8,128)(2,1)}, bf16[3,160,128]{2,1,0:T(8,128)(2,1)S(1)}, u32[]{:S(2)}, u32[]{:S(2)}) collective-permute-start(bf16[3,160,128]{2,1,0:T(8,128)(2,1)} %get-tuple-element.23), channel_id=1, source_target_pairs={{0,2},{1,3},{2,0},{3,1},{4,6},{5,7},{6,4},{7,5},{8,10},{9,11},{10,... | collective-permute-start | bytes 368648 | tf_op jit(solution)/shard_map/ppermute | solution.py:233
  15.8 0.4 collective-permute-start.2
  16.2 1.4 collective-permute-start.3
  17.5 0.3 collective-permute-start.4
  17.8 0.0 collective-permute-done.refs_1_
  17.8 2.4 %collective-permute-start.5 = (bf16[3,160,128]{2,1,0:T(8,128)(2,1)}, bf16[3,160,128]{2,1,0:T(8,128)(2,1)S(1)}, u32[]{:S(2)}, u32[]{:S(2)}) collective-permute-start(bf16[3,160,128]{2,1,0:T(8,128)(2,1)} %get-tuple-element.27), channel_id=1, source_target_pairs={{0,6},{1,7},{2,4},{3,5},{4,2},{5,3},{6,0},{7,1},{8,14},{9,15},{10,... | collective-permute-start | bytes 368648 | tf_op jit(solution)/shard_map/ppermute | solution.py:233
  20.2 6.4 %collective-permute-done.1.refs_2_ = bf16[3,160,128]{2,1,0:T(8,128)(2,1)S(1)} collective-permute-done((bf16[3,160,128]{2,1,0:T(8,128)(2,1)}, bf16[3,160,128]{2,1,0:T(8,128)(2,1)S(1)}, u32[]{:S(2)}, u32[]{:S(2)}) %collective-permute-start.1) | collective-permute-done | bytes 122912 | tf_op jit(solution)/shard_map/ppermute | solution.py:233
  26.6 1.6 collective-permute-start.6
  28.2 5.3 %collective-permute-done.2.refs_3_ = bf16[3,160,128]{2,1,0:T(8,128)(2,1)S(1)} collective-permute-done((bf16[3,160,128]{2,1,0:T(8,128)(2,1)}, bf16[3,160,128]{2,1,0:T(8,128)(2,1)S(1)}, u32[]{:S(2)}, u32[]{:S(2)}) %collective-permute-start.2) | collective-permute-done | bytes 122912 | tf_op jit(solution)/shard_map/ppermute | solution.py:233
  33.5 0.0 collective-permute-start.7
  33.5 11.8 %collective-permute-done.3.refs_4_ = bf16[3,160,128]{2,1,0:T(8,128)(2,1)S(1)} collective-permute-done((bf16[3,160,128]{2,1,0:T(8,128)(2,1)}, bf16[3,160,128]{2,1,0:T(8,128)(2,1)S(1)}, u32[]{:S(2)}, u32[]{:S(2)}) %collective-permute-start.3) | collective-permute-done | bytes 122912 | tf_op jit(solution)/shard_map/ppermute | solution.py:233
  45.3 5.0 %collective-permute-start.8 = (bf16[3,160,128]{2,1,0:T(8,128)(2,1)}, bf16[3,160,128]{2,1,0:T(8,128)(2,1)S(1)}, u32[]{:S(2)}, u32[]{:S(2)}) collective-permute-start(bf16[3,160,128]{2,1,0:T(8,128)(2,1)} %get-tuple-element.30), channel_id=1, source_target_pairs={{0,9},{1,8},{2,11},{3,10},{4,13},{5,12},{6,15},{7,14},{8,1},{9,0},... | collective-permute-start | bytes 368648 | tf_op jit(solution)/shard_map/ppermute | solution.py:233
  50.3 0.0 collective-permute-done.4.refs_5_
  50.3 3.4 %collective-permute-start.9 = (bf16[3,160,128]{2,1,0:T(8,128)(2,1)}, bf16[3,160,128]{2,1,0:T(8,128)(2,1)S(1)}, u32[]{:S(2)}, u32[]{:S(2)}) collective-permute-start(bf16[3,160,128]{2,1,0:T(8,128)(2,1)} %get-tuple-element.31), channel_id=1, source_target_pairs={{0,10},{1,11},{2,8},{3,9},{4,14},{5,15},{6,12},{7,13},{8,2},{9,3},... | collective-permute-start | bytes 368648 | tf_op jit(solution)/shard_map/ppermute | solution.py:233
  53.7 0.0 collective-permute-done.5.refs_6_
  53.7 2.8 %collective-permute-start.10 = (bf16[3,160,128]{2,1,0:T(8,128)(2,1)}, bf16[3,160,128]{2,1,0:T(8,128)(2,1)S(1)}, u32[]{:S(2)}, u32[]{:S(2)}) collective-permute-start(bf16[3,160,128]{2,1,0:T(8,128)(2,1)} %get-tuple-element.32), channel_id=1, source_target_pairs={{0,11},{1,10},{2,9},{3,8},{4,15},{5,14},{6,13},{7,12},{8,3},{9,2},... | collective-permute-start | bytes 368648 | tf_op jit(solution)/shard_map/ppermute | solution.py:233
  56.5 0.0 collective-permute-done.6.refs_7_
  56.5 1.3 collective-permute-start.11
  57.8 14.4 %collective-permute-done.7.refs_8_ = bf16[3,160,128]{2,1,0:T(8,128)(2,1)S(1)} collective-permute-done((bf16[3,160,128]{2,1,0:T(8,128)(2,1)}, bf16[3,160,128]{2,1,0:T(8,128)(2,1)S(1)}, u32[]{:S(2)}, u32[]{:S(2)}) %collective-permute-start.7) | collective-permute-done | bytes 122912 | tf_op jit(solution)/shard_map/ppermute | solution.py:233
  72.2 1.8 %collective-permute-start.12 = (bf16[3,160,128]{2,1,0:T(8,128)(2,1)}, bf16[3,160,128]{2,1,0:T(8,128)(2,1)}, u32[]{:S(2)}, u32[]{:S(2)}) collective-permute-start(bf16[3,160,128]{2,1,0:T(8,128)(2,1)} %get-tuple-element.34), channel_id=1, source_target_pairs={{0,13},{1,12},{2,15},{3,14},{4,9},{5,8},{6,11},{7,10},{8,5},{9,4},... | collective-permute-start | bytes 368648 | tf_op jit(solution)/shard_map/ppermute | solution.py:233
  74.0 1.6 %collective-permute-done.8.refs_9_ = bf16[3,160,128]{2,1,0:T(8,128)(2,1)S(1)} collective-permute-done((bf16[3,160,128]{2,1,0:T(8,128)(2,1)}, bf16[3,160,128]{2,1,0:T(8,128)(2,1)S(1)}, u32[]{:S(2)}, u32[]{:S(2)}) %collective-permute-start.8) | collective-permute-done | bytes 122912 | tf_op jit(solution)/shard_map/ppermute | solution.py:233
  75.7 2.6 %collective-permute-start.13 = (bf16[3,160,128]{2,1,0:T(8,128)(2,1)}, bf16[3,160,128]{2,1,0:T(8,128)(2,1)}, u32[]{:S(2)}, u32[]{:S(2)}) collective-permute-start(bf16[3,160,128]{2,1,0:T(8,128)(2,1)} %get-tuple-element.35), channel_id=1, source_target_pairs={{0,14},{1,15},{2,12},{3,13},{4,10},{5,11},{6,8},{7,9},{8,6},{9,7},... | collective-permute-start | bytes 368648 | tf_op jit(solution)/shard_map/ppermute | solution.py:233
  78.2 2.7 %collective-permute-done.9.refs_10_ = bf16[3,160,128]{2,1,0:T(8,128)(2,1)S(1)} collective-permute-done((bf16[3,160,128]{2,1,0:T(8,128)(2,1)}, bf16[3,160,128]{2,1,0:T(8,128)(2,1)S(1)}, u32[]{:S(2)}, u32[]{:S(2)}) %collective-permute-start.9) | collective-permute-done | bytes 122912 | tf_op jit(solution)/shard_map/ppermute | solution.py:233
  80.9 1.9 %collective-permute-start.14 = (bf16[3,160,128]{2,1,0:T(8,128)(2,1)}, bf16[3,160,128]{2,1,0:T(8,128)(2,1)}, u32[]{:S(2)}, u32[]{:S(2)}) collective-permute-start(bf16[3,160,128]{2,1,0:T(8,128)(2,1)} %get-tuple-element.36), channel_id=1, source_target_pairs={{0,15},{1,14},{2,13},{3,12},{4,11},{5,10},{6,9},{7,8},{8,7},{9,6},... | collective-permute-start | bytes 368648 | tf_op jit(solution)/shard_map/ppermute | solution.py:233
  82.8 5.6 %collective-permute-done.10.refs_11_ = bf16[3,160,128]{2,1,0:T(8,128)(2,1)S(1)} collective-permute-done((bf16[3,160,128]{2,1,0:T(8,128)(2,1)}, bf16[3,160,128]{2,1,0:T(8,128)(2,1)S(1)}, u32[]{:S(2)}, u32[]{:S(2)}) %collective-permute-start.10) | collective-permute-done | bytes 122912 | tf_op jit(solution)/shard_map/ppermute | solution.py:233
  88.4 0.0 collective-permute-done.11.refs_12_
  88.4 0.0 collective-permute-done.12.refs_13_
  88.4 0.0 collective-permute-done.13.refs_14_
  88.4 0.0 collective-permute-done.14.refs_15_
  88.4 0.0 copy-done.2
  88.4 0.0 copy-done.3
  88.4 0.0 copy-done.4
  88.4 0.0 copy-done.5
  88.5 0.0 copy-done.6
  88.5 0.0 copy-done.7
  88.5 0.5 copy-done.12
  89.0 0.1 copy-done.13
  89.1 15.6 %attend_parts.1 = bf16[2560,128]{1,0:T(8,128)(2,1)} custom-call(s32[5]{0:T(128)} %rank_ref.3, s32[5]{0:T(128)} %ends_ref.3, s32[1]{0:T(128)} %bitcast.1.me_ref, bf16[3,160,128]{2,1,0:T(8,128)(2,1)} %get-tuple-element.21.refs_0_, bf16[3,160,128]{2,1,0:T(8,128)(2,1)} %copy-done.2, bf16[3,160,128]{2,1,0:T(8,128)(2,1)} %copy-done.3, ...), custom_call_target="tpu_custom_call" | custom-call | tf_op jit(solution)/shard_map/attend_parts/pallas_call | solution.py:122
  104.7 0.0 all-to-all-done.q_ref.kf_ref.vf_ref
  104.7 13.0 %all-to-all-start.2 = ((bf16[16,160,128]{2,1,0:T(8,128)(2,1)}), bf16[16,160,128]{2,1,0:T(8,128)(2,1)S(1)}, u32[]{:S(2)}, u32[]{:S(2)}) async-start(bf16[16,160,128]{2,1,0:T(8,128)(2,1)} %bitcast.4), calls=%async_computation.2 | async-start | bytes 1310720 | tf_op jit(solution)/shard_map/all_to_all | solution.py:226
  117.7 15.3 %attend_whole.1 = bf16[2560,128]{1,0:T(8,128)(2,1)} custom-call(s32[5]{0:T(128)} %rank_ref.3, s32[5]{0:T(128)} %ends_ref.3, bf16[16,3,160,128]{3,2,1,0:T(8,128)(2,1)} %copy-done, bf16[16,3,160,128]{3,2,1,0:T(8,128)(2,1)} %copy-done, bf16[16,3,160,128]{3,2,1,0:T(8,128)(2,1)} %copy-done, bf16[2560,256]{1,0:T(8,128)(2,1)} %refs_16_.1, bf16[2560,256]{1,0:T(8,128)(2,1)} %refs_17_.1), custom_call_target="tpu_custom_call" | custom-call | tf_op jit(solution)/shard_map/attend_whole/pallas_call | solution.py:86
  133.0 1.0 all-to-all-done.2.refs_1_
  134.1 23.3 %all_to_all.15.refs_0_ = bf16[16,160,128]{2,1,0:T(8,128)(2,1)} all-to-all(bf16[16,160,128]{2,1,0:T(8,128)(2,1)} %bitcast.3), channel_id=1, replica_groups=mesh['groups'=2,'seq'=16] {'seq'}, dimensions={0} | all-to-all | bytes 1310720 | tf_op jit(solution)/shard_map/all_to_all | solution.py:226
  157.4 2.3 %unpack.1 = bf16[160,4096]{1,0:T(8,128)(2,1)} custom-call(bf16[16,160,128]{2,1,0:T(8,128)(2,1)} %all_to_all.15.refs_0_, bf16[16,160,128]{2,1,0:T(8,128)(2,1)} %copy-done.1), custom_call_target="tpu_custom_call" | custom-call | tf_op jit(solution)/shard_map/unpack/pallas_call | solution.py:208
  (20 shorter events, 0.0 us)
Async XLA Ops:
  2.8 101.9 %all-to-all-start = ((bf16[16,3,160,128]{3,2,1,0:T(8,128)(2,1)}), bf16[16,3,160,128]{3,2,1,0:T(8,128)(2,1)S(1)}, u32[]{:S(2)}, u32[]{:S(2)}) async-start(bf16[16,3,160,128]{3,2,1,0:T(8,128)(2,1)} %pack.1), calls=%async_computation | async-start | bytes 3932160 | tf_op jit(solution)/shard_map/all_to_all | solution.py:226
  14.0 3.8 %collective-permute-start = (bf16[3,160,128]{2,1,0:T(8,128)(2,1)}, bf16[3,160,128]{2,1,0:T(8,128)(2,1)S(1)}, u32[]{:S(2)}, u32[]{:S(2)}) collective-permute-start(bf16[3,160,128]{2,1,0:T(8,128)(2,1)} %get-tuple-element.22), channel_id=1, source_target_pairs={{0,1},{1,0},{2,3},{3,2},{4,5},{5,4},{6,7},{7,6},{8,9},{9,8},{10,11... | collective-permute-start | bytes 368648 | tf_op jit(solution)/shard_map/ppermute | solution.py:233
  14.1 12.5 %collective-permute-start.1 = (bf16[3,160,128]{2,1,0:T(8,128)(2,1)}, bf16[3,160,128]{2,1,0:T(8,128)(2,1)S(1)}, u32[]{:S(2)}, u32[]{:S(2)}) collective-permute-start(bf16[3,160,128]{2,1,0:T(8,128)(2,1)} %get-tuple-element.23), channel_id=1, source_target_pairs={{0,2},{1,3},{2,0},{3,1},{4,6},{5,7},{6,4},{7,5},{8,10},{9,11},{10,... | collective-permute-start | bytes 368648 | tf_op jit(solution)/shard_map/ppermute | solution.py:233
  15.8 17.7 %collective-permute-start.2 = (bf16[3,160,128]{2,1,0:T(8,128)(2,1)}, bf16[3,160,128]{2,1,0:T(8,128)(2,1)S(1)}, u32[]{:S(2)}, u32[]{:S(2)}) collective-permute-start(bf16[3,160,128]{2,1,0:T(8,128)(2,1)} %get-tuple-element.24), channel_id=1, source_target_pairs={{0,3},{1,2},{2,1},{3,0},{4,7},{5,6},{6,5},{7,4},{8,11},{9,10},{10,... | collective-permute-start | bytes 368648 | tf_op jit(solution)/shard_map/ppermute | solution.py:233
  16.2 29.1 %collective-permute-start.3 = (bf16[3,160,128]{2,1,0:T(8,128)(2,1)}, bf16[3,160,128]{2,1,0:T(8,128)(2,1)S(1)}, u32[]{:S(2)}, u32[]{:S(2)}) collective-permute-start(bf16[3,160,128]{2,1,0:T(8,128)(2,1)} %get-tuple-element.25), channel_id=1, source_target_pairs={{0,4},{1,5},{2,6},{3,7},{4,0},{5,1},{6,2},{7,3},{8,12},{9,13},{10,... | collective-permute-start | bytes 368648 | tf_op jit(solution)/shard_map/ppermute | solution.py:233
  17.5 32.8 %collective-permute-start.4 = (bf16[3,160,128]{2,1,0:T(8,128)(2,1)}, bf16[3,160,128]{2,1,0:T(8,128)(2,1)S(1)}, u32[]{:S(2)}, u32[]{:S(2)}) collective-permute-start(bf16[3,160,128]{2,1,0:T(8,128)(2,1)} %get-tuple-element.26), channel_id=1, source_target_pairs={{0,5},{1,4},{2,7},{3,6},{4,1},{5,0},{6,3},{7,2},{8,13},{9,12},{10,... | collective-permute-start | bytes 368648 | tf_op jit(solution)/shard_map/ppermute | solution.py:233
  17.8 70.6 %copy-start.2 = (bf16[3,160,128]{2,1,0:T(8,128)(2,1)}, bf16[3,160,128]{2,1,0:T(8,128)(2,1)S(1)}, u32[]{:S(2)}) copy-start(bf16[3,160,128]{2,1,0:T(8,128)(2,1)S(1)} %collective-permute-done.refs_1_) | copy-start | bytes 368644
  17.8 35.9 %collective-permute-start.5 = (bf16[3,160,128]{2,1,0:T(8,128)(2,1)}, bf16[3,160,128]{2,1,0:T(8,128)(2,1)S(1)}, u32[]{:S(2)}, u32[]{:S(2)}) collective-permute-start(bf16[3,160,128]{2,1,0:T(8,128)(2,1)} %get-tuple-element.27), channel_id=1, source_target_pairs={{0,6},{1,7},{2,4},{3,5},{4,2},{5,3},{6,0},{7,1},{8,14},{9,15},{10,... | collective-permute-start | bytes 368648 | tf_op jit(solution)/shard_map/ppermute | solution.py:233
  26.6 61.8 %copy-start.3 = (bf16[3,160,128]{2,1,0:T(8,128)(2,1)}, bf16[3,160,128]{2,1,0:T(8,128)(2,1)S(1)}, u32[]{:S(2)}) copy-start(bf16[3,160,128]{2,1,0:T(8,128)(2,1)S(1)} %collective-permute-done.1.refs_2_) | copy-start | bytes 368644
  26.6 29.9 %collective-permute-start.6 = (bf16[3,160,128]{2,1,0:T(8,128)(2,1)}, bf16[3,160,128]{2,1,0:T(8,128)(2,1)S(1)}, u32[]{:S(2)}, u32[]{:S(2)}) collective-permute-start(bf16[3,160,128]{2,1,0:T(8,128)(2,1)} %get-tuple-element.28), channel_id=1, source_target_pairs={{0,7},{1,6},{2,5},{3,4},{4,3},{5,2},{6,1},{7,0},{8,15},{9,14},{10,... | collective-permute-start | bytes 368648 | tf_op jit(solution)/shard_map/ppermute | solution.py:233
  33.5 55.0 %copy-start.4 = (bf16[3,160,128]{2,1,0:T(8,128)(2,1)}, bf16[3,160,128]{2,1,0:T(8,128)(2,1)S(1)}, u32[]{:S(2)}) copy-start(bf16[3,160,128]{2,1,0:T(8,128)(2,1)S(1)} %collective-permute-done.2.refs_3_) | copy-start | bytes 368644
  33.5 38.7 %collective-permute-start.7 = (bf16[3,160,128]{2,1,0:T(8,128)(2,1)}, bf16[3,160,128]{2,1,0:T(8,128)(2,1)S(1)}, u32[]{:S(2)}, u32[]{:S(2)}) collective-permute-start(bf16[3,160,128]{2,1,0:T(8,128)(2,1)} %get-tuple-element.29), channel_id=1, source_target_pairs={{0,8},{1,9},{2,10},{3,11},{4,12},{5,13},{6,14},{7,15},{8,0},{9,1},... | collective-permute-start | bytes 368648 | tf_op jit(solution)/shard_map/ppermute | solution.py:233
  45.3 43.2 %copy-start.5 = (bf16[3,160,128]{2,1,0:T(8,128)(2,1)}, bf16[3,160,128]{2,1,0:T(8,128)(2,1)S(1)}, u32[]{:S(2)}) copy-start(bf16[3,160,128]{2,1,0:T(8,128)(2,1)S(1)} %collective-permute-done.3.refs_4_) | copy-start | bytes 368644
  45.3 30.4 %collective-permute-start.8 = (bf16[3,160,128]{2,1,0:T(8,128)(2,1)}, bf16[3,160,128]{2,1,0:T(8,128)(2,1)S(1)}, u32[]{:S(2)}, u32[]{:S(2)}) collective-permute-start(bf16[3,160,128]{2,1,0:T(8,128)(2,1)} %get-tuple-element.30), channel_id=1, source_target_pairs={{0,9},{1,8},{2,11},{3,10},{4,13},{5,12},{6,15},{7,14},{8,1},{9,0},... | collective-permute-start | bytes 368648 | tf_op jit(solution)/shard_map/ppermute | solution.py:233
  50.3 38.1 %copy-start.6 = (bf16[3,160,128]{2,1,0:T(8,128)(2,1)}, bf16[3,160,128]{2,1,0:T(8,128)(2,1)S(1)}, u32[]{:S(2)}) copy-start(bf16[3,160,128]{2,1,0:T(8,128)(2,1)S(1)} %collective-permute-done.4.refs_5_) | copy-start | bytes 368644
  50.3 30.6 %collective-permute-start.9 = (bf16[3,160,128]{2,1,0:T(8,128)(2,1)}, bf16[3,160,128]{2,1,0:T(8,128)(2,1)S(1)}, u32[]{:S(2)}, u32[]{:S(2)}) collective-permute-start(bf16[3,160,128]{2,1,0:T(8,128)(2,1)} %get-tuple-element.31), channel_id=1, source_target_pairs={{0,10},{1,11},{2,8},{3,9},{4,14},{5,15},{6,12},{7,13},{8,2},{9,3},... | collective-permute-start | bytes 368648 | tf_op jit(solution)/shard_map/ppermute | solution.py:233
  53.7 34.8 %copy-start.7 = (bf16[3,160,128]{2,1,0:T(8,128)(2,1)}, bf16[3,160,128]{2,1,0:T(8,128)(2,1)S(1)}, u32[]{:S(2)}) copy-start(bf16[3,160,128]{2,1,0:T(8,128)(2,1)S(1)} %collective-permute-done.5.refs_6_) | copy-start | bytes 368644
  53.7 34.7 %collective-permute-start.10 = (bf16[3,160,128]{2,1,0:T(8,128)(2,1)}, bf16[3,160,128]{2,1,0:T(8,128)(2,1)S(1)}, u32[]{:S(2)}, u32[]{:S(2)}) collective-permute-start(bf16[3,160,128]{2,1,0:T(8,128)(2,1)} %get-tuple-element.32), channel_id=1, source_target_pairs={{0,11},{1,10},{2,9},{3,8},{4,15},{5,14},{6,13},{7,12},{8,3},{9,2},... | collective-permute-start | bytes 368648 | tf_op jit(solution)/shard_map/ppermute | solution.py:233
  56.5 32.0 %copy-start.8 = (bf16[3,160,128]{2,1,0:T(8,128)(2,1)}, bf16[3,160,128]{2,1,0:T(8,128)(2,1)S(1)}, u32[]{:S(2)}) copy-start(bf16[3,160,128]{2,1,0:T(8,128)(2,1)S(1)} %collective-permute-done.6.refs_7_) | copy-start | bytes 368644
  56.5 31.9 %collective-permute-start.11 = (bf16[3,160,128]{2,1,0:T(8,128)(2,1)}, bf16[3,160,128]{2,1,0:T(8,128)(2,1)S(1)}, u32[]{:S(2)}, u32[]{:S(2)}) collective-permute-start(bf16[3,160,128]{2,1,0:T(8,128)(2,1)} %get-tuple-element.33), channel_id=1, source_target_pairs={{0,12},{1,13},{2,14},{3,15},{4,8},{5,9},{6,10},{7,11},{8,4},{9,5},... | collective-permute-start | bytes 368648 | tf_op jit(solution)/shard_map/ppermute | solution.py:233
  72.2 16.3 %copy-start.9 = (bf16[3,160,128]{2,1,0:T(8,128)(2,1)}, bf16[3,160,128]{2,1,0:T(8,128)(2,1)S(1)}, u32[]{:S(2)}) copy-start(bf16[3,160,128]{2,1,0:T(8,128)(2,1)S(1)} %collective-permute-done.7.refs_8_) | copy-start | bytes 368644
  72.2 16.2 %collective-permute-start.12 = (bf16[3,160,128]{2,1,0:T(8,128)(2,1)}, bf16[3,160,128]{2,1,0:T(8,128)(2,1)}, u32[]{:S(2)}, u32[]{:S(2)}) collective-permute-start(bf16[3,160,128]{2,1,0:T(8,128)(2,1)} %get-tuple-element.34), channel_id=1, source_target_pairs={{0,13},{1,12},{2,15},{3,14},{4,9},{5,8},{6,11},{7,10},{8,5},{9,4},... | collective-permute-start | bytes 368648 | tf_op jit(solution)/shard_map/ppermute | solution.py:233
  75.7 12.8 %copy-start.10 = (bf16[3,160,128]{2,1,0:T(8,128)(2,1)}, bf16[3,160,128]{2,1,0:T(8,128)(2,1)S(1)}, u32[]{:S(2)}) copy-start(bf16[3,160,128]{2,1,0:T(8,128)(2,1)S(1)} %collective-permute-done.8.refs_9_) | copy-start | bytes 368644
  75.7 12.7 %collective-permute-start.13 = (bf16[3,160,128]{2,1,0:T(8,128)(2,1)}, bf16[3,160,128]{2,1,0:T(8,128)(2,1)}, u32[]{:S(2)}, u32[]{:S(2)}) collective-permute-start(bf16[3,160,128]{2,1,0:T(8,128)(2,1)} %get-tuple-element.35), channel_id=1, source_target_pairs={{0,14},{1,15},{2,12},{3,13},{4,10},{5,11},{6,8},{7,9},{8,6},{9,7},... | collective-permute-start | bytes 368648 | tf_op jit(solution)/shard_map/ppermute | solution.py:233
  80.9 7.6 %copy-start.11 = (bf16[3,160,128]{2,1,0:T(8,128)(2,1)}, bf16[3,160,128]{2,1,0:T(8,128)(2,1)S(1)}, u32[]{:S(2)}) copy-start(bf16[3,160,128]{2,1,0:T(8,128)(2,1)S(1)} %collective-permute-done.9.refs_10_) | copy-start | bytes 368644
  80.9 7.5 %collective-permute-start.14 = (bf16[3,160,128]{2,1,0:T(8,128)(2,1)}, bf16[3,160,128]{2,1,0:T(8,128)(2,1)}, u32[]{:S(2)}, u32[]{:S(2)}) collective-permute-start(bf16[3,160,128]{2,1,0:T(8,128)(2,1)} %get-tuple-element.36), channel_id=1, source_target_pairs={{0,15},{1,14},{2,13},{3,12},{4,11},{5,10},{6,9},{7,8},{8,7},{9,6},... | collective-permute-start | bytes 368648 | tf_op jit(solution)/shard_map/ppermute | solution.py:233
  88.4 0.7 copy-start.12
  88.4 0.7 copy-start.13
  104.7 13.0 %copy-start = (bf16[16,3,160,128]{3,2,1,0:T(8,128)(2,1)}, bf16[16,3,160,128]{3,2,1,0:T(8,128)(2,1)S(1)}, u32[]{:S(2)}) copy-start(bf16[16,3,160,128]{3,2,1,0:T(8,128)(2,1)S(1)} %all-to-all-done.q_ref.kf_ref.vf_ref) | copy-start | bytes 5898244
  104.7 29.3 %all-to-all-start.2 = ((bf16[16,160,128]{2,1,0:T(8,128)(2,1)}), bf16[16,160,128]{2,1,0:T(8,128)(2,1)S(1)}, u32[]{:S(2)}, u32[]{:S(2)}) async-start(bf16[16,160,128]{2,1,0:T(8,128)(2,1)} %bitcast.4), calls=%async_computation.2 | async-start | bytes 1310720 | tf_op jit(solution)/shard_map/all_to_all | solution.py:226
  134.1 23.3 %copy-start.1 = (bf16[16,160,128]{2,1,0:T(8,128)(2,1)}, bf16[16,160,128]{2,1,0:T(8,128)(2,1)S(1)}, u32[]{:S(2)}) copy-start(bf16[16,160,128]{2,1,0:T(8,128)(2,1)S(1)} %all-to-all-done.2.refs_1_) | copy-start | bytes 1966084

commit v4 on v3

--- a/solution.py
+++ b/solution.py
@@ -13,24 +13,38 @@
 PATCH = 512
 
 
-def attend_patch(p, rank_ref, ends_ref, query, k_ref, v_ref, ks_ref, vs_ref, out_ref, scratch):
+def attend_all(rank_ref, ends_ref, q_ref, k_ref, v_ref, ks_ref, vs_ref, out_ref, scratch):
     even, odd, top, total, mixed = scratch
     factor = math.log2(math.e) / math.sqrt(HEAD_DIM)
-    mine = rank_ref[p]
-    count = ends_ref[p] // PATCH
-    top[...] = jnp.full(top.shape, -jnp.inf, jnp.float32)
-    total[...] = jnp.zeros(total.shape, jnp.float32)
-    mixed[...] = jnp.zeros(mixed.shape, jnp.float32)
-
-    def chosen(j, new_ref, old_ref):
-        at = pl.ds(pl.multiple_of(j * PATCH, PATCH), PATCH)
-        return jnp.where(rank_ref[j] <= mine, new_ref[at, :], old_ref[at, :])
-
-    def score(j):
-        keys = chosen(jnp.minimum(j, count - 1), k_ref, ks_ref)
-        return lax.dot_general(query, keys, (((1,), (1,)), ((), ())), preferred_element_type=jnp.float32)
-
-    def fold(scores, j):
+    patches = rank_ref.shape[0]
+
+    def rows_of(patch):
+        return pl.ds(pl.multiple_of(patch * PATCH, PATCH), PATCH)
+
+    def blocks_of(p):
+        return ends_ref[p] // PATCH
+
+    def chosen(p, j, new_ref, old_ref):
+        return jnp.where(rank_ref[j] <= rank_ref[p], new_ref[rows_of(j), :], old_ref[rows_of(j), :])
+
+    def after(p, j):
+        last = j + 1 >= blocks_of(p)
+        return jnp.where(last, jnp.minimum(p + 1, patches - 1), p), jnp.where(last, 0, j + 1)
+
+    def score(scores, p, j):
+        scores[...] = lax.dot_general(
+            q_ref[rows_of(p), :],
+            chosen(p, j, k_ref, ks_ref),
+            (((1,), (1,)), ((), ())),
+            preferred_element_type=jnp.float32,
+        )
+
+    def clear():
+        top[...] = jnp.full(top.shape, -jnp.inf, jnp.float32)
+        total[...] = jnp.zeros(total.shape, jnp.float32)
+        mixed[...] = jnp.zeros(mixed.shape, jnp.float32)
+
+    def fold(scores, p, j):
         before = top[...]
         higher = jnp.maximum(before, jnp.max(scores[...], axis=1, keepdims=True) * factor)
         top[...] = higher
@@ -44,35 +58,43 @@
         total[...] = sums
         weights = jnp.concatenate(rounded, axis=1)
         mixed[...] = mixed[...] * shrink + jnp.dot(
-            weights, chosen(j, v_ref, vs_ref), preferred_element_type=jnp.float32
+            weights, chosen(p, j, v_ref, vs_ref), preferred_element_type=jnp.float32
         )
 
-    even[...] = score(0)
-
-    def two(t, _):
-        odd[...] = score(2 * t + 1)
-        fold(even, 2 * t)
-
-        @pl.when(2 * t + 1 < count)
+        @pl.when(j + 1 == blocks_of(p))
         def _():
-            even[...] = score(2 * t + 2)
-            fold(odd, 2 * t + 1)
-
-        return 0
-
-    lax.fori_loop(0, (count + 1) // 2, two, 0)
-    out_ref[...] = (mixed[...] / jnp.sum(total[...], axis=1, keepdims=True)).astype(jnp.bfloat16)
+            out_ref[rows_of(p), :] = (mixed[...] / jnp.sum(total[...], axis=1, keepdims=True)).astype(jnp.bfloat16)
+            clear()
+
+    pairs = blocks_of(0)
+    for p in range(1, patches):
+        pairs = pairs + blocks_of(p)
+    clear()
+    score(even, 0, 0)
+
+    def two(t, at):
+        then = after(*at)
+        score(odd, *then)
+        fold(even, *at)
+        beyond = after(*then)
+
+        @pl.when(2 * t + 1 < pairs)
+        def _():
+            score(even, *beyond)
+            fold(odd, *then)
+
+        return beyond
+
+    lax.fori_loop(0, (pairs + 1) // 2, two, (jnp.int32(0), jnp.int32(0)))
 
 
 ATTEND_SCRATCH = [pltpu.VMEM((PATCH, PATCH), jnp.float32)] * 2 + [pltpu.VMEM((PATCH, HEAD_DIM), jnp.float32)] * 3
 
 
 def attend_whole_kernel(rank_ref, ends_ref, q_ref, kf_ref, vf_ref, ks_ref, vs_ref, out_ref, *scratch):
-    p = pl.program_id(0)
     flat = (q_ref.shape[0] * q_ref.shape[1], HEAD_DIM)
-    query = q_ref.reshape(*flat)[pl.ds(pl.multiple_of(p * PATCH, PATCH), PATCH), :]
-    keys, values = kf_ref.reshape(*flat), vf_ref.reshape(*flat)
-    attend_patch(p, rank_ref, ends_ref, query, keys, values, ks_ref, vs_ref, out_ref, scratch)
+    fresh = [ref.reshape(*flat) for ref in (q_ref, kf_ref, vf_ref)]
+    attend_all(rank_ref, ends_ref, *fresh, ks_ref, vs_ref, out_ref, scratch)
 
 
 def attend_whole(packed, k_stale, v_stale, rank, ends, head):
@@ -87,9 +109,9 @@
         attend_whole_kernel,
         grid_spec=pltpu.PrefetchScalarGridSpec(
             num_scalar_prefetch=2,
-            grid=(rank.shape[0],),
+            grid=(1,),
             in_specs=[*part, stale, stale],
-            out_specs=pl.BlockSpec((PATCH, HEAD_DIM), lambda p, r, e: (p, 0)),
+            out_specs=pl.BlockSpec((total_rows, HEAD_DIM), lambda p, r, e: (0, 0)),
             scratch_shapes=ATTEND_SCRATCH,
         ),
         out_shape=jax.ShapeDtypeStruct((total_rows, HEAD_DIM), jnp.bfloat16),
@@ -99,19 +121,13 @@
 
 def attend_parts_kernel(rank_ref, ends_ref, me_ref, *refs, peers):
     blocks = refs[:peers]
-    ks_ref, vs_ref, out_ref, q_all, k_all, v_all, *scratch = refs[peers:]
-    p = pl.program_id(0)
+    ks_ref, vs_ref, out_ref, *fresh = refs[peers:peers + 6]
     rows_here = blocks[0].shape[1]
-
-    @pl.when(p == 0)
-    def _():
-        for k in range(peers):
-            at = pl.ds(pl.multiple_of((me_ref[0] ^ k) * rows_here, rows_here), rows_here)
-            for i, ref in enumerate((q_all, k_all, v_all)):
-                ref[at, :] = blocks[k][i]
-
-    query = q_all[pl.ds(pl.multiple_of(p * PATCH, PATCH), PATCH), :]
-    attend_patch(p, rank_ref, ends_ref, query, k_all, v_all, ks_ref, vs_ref, out_ref, scratch)
+    for k in range(peers):
+        at = pl.ds(pl.multiple_of((me_ref[0] ^ k) * rows_here, rows_here), rows_here)
+        for i, ref in enumerate(fresh):
+            ref[at, :] = blocks[k][i]
+    attend_all(rank_ref, ends_ref, *fresh, ks_ref, vs_ref, out_ref, refs[peers + 6:])
 
 
 def attend_parts(blocks, k_stale, v_stale, rank, ends, me, head):
@@ -123,9 +139,9 @@
         functools.partial(attend_parts_kernel, peers=peers),
         grid_spec=pltpu.PrefetchScalarGridSpec(
             num_scalar_prefetch=3,
-            grid=(rank.shape[0],),
+            grid=(1,),
             in_specs=[pl.BlockSpec(blocks[0].shape, lambda p, r, e, m: (0, 0, 0))] * peers + [stale, stale],
-            out_specs=pl.BlockSpec((PATCH, HEAD_DIM), lambda p, r, e, m: (p, 0)),
+            out_specs=pl.BlockSpec((total_rows, HEAD_DIM), lambda p, r, e, m: (0, 0)),
             scratch_shapes=[pltpu.VMEM((total_rows, HEAD_DIM), jnp.bfloat16)] * 3 + ATTEND_SCRATCH,
         ),
         out_shape=jax.ShapeDtypeStruct((total_rows, HEAD_DIM), jnp.bfloat16),

time: 161 us -> 159 us (0.988)
  Pallas kernels: 39.9 us -> 37.6 us
  transfers between devices with their start and end apart: 17 -> 17, of which waited for: 8 -> 8; matrix products, arithmetic and copies ran while one was open for 0% -> 0% of each run, Pallas kernels for 22% -> 20%
where the time goes in v4:
time: 159 us
  waiting for transfers between devices  50 us (31%)
  starting transfers between devices  46.9 us (29%)
  Pallas kernels  37.6 us (24%)
  blocking collectives  23.4 us (15%)
    ppermute x15, waiting for transfers between devices, shards(): lax.ppermute(blocks[k], 'seq', [(s, s ^ k) for s in range(peers)])  47.9 us
    ppermute x15, starting transfers between devices, shards(): lax.ppermute(blocks[k], 'seq', [(s, s ^ k) for s in range(peers)])  26.5 us
    all_to_all x1, blocking collectives, swap(): return lax.all_to_all(array, 'seq', split_axis=0, concat_axis=0, tiled=True)  23.4 us
    all_to_all x2, starting transfers between devices, swap(): return lax.all_to_all(array, 'seq', split_axis=0, concat_axis=0, tiled=True)  20.4 us
    pallas_call x1, Pallas kernels, attend_parts(): pl.pallas_call(functools.partial(attend_parts_kernel, peers=peers), grid_...  14.4 us
    pallas_call x1, Pallas kernels, attend_whole(): pl.pallas_call(attend_whole_kernel, grid_spec=pltpu.PrefetchScalarGridSpe...  14.2 us
    pallas_call x1, Pallas kernels, split(): pl.pallas_call(functools.partial(split_kernel, head=head, heads_here=head...  3.86 us
  transfers between devices with their start and end apart: 17, of which 8 were waited for; matrix products, arithmetic and copies ran while one was open for 0% of the time, Pallas kernels for 20%

profile of v4, /device:TPU:1, one launch (start us, length us, event | category | flops | bytes accessed | tf_op | source)
XLA Modules:
  0.0 158.5 jit_solution(5671007626102020573)
XLA Ops:
  0.0 2.8 %pack.1 = bf16[16,3,160,128]{3,2,1,0:T(8,128)(2,1)} custom-call(bf16[160,4096]{1,0:T(8,128)(2,1)} %q_ref.3, bf16[160,4096]{1,0:T(8,128)(2,1)} %k_ref.3, bf16[160,4096]{1,0:T(8,128)(2,1)} %v_ref.3), custom_call_target="tpu_custom_call" | custom-call | tf_op jit(solution)/shard_map/pack/pallas_call | solution.py:174
  2.8 7.4 %all-to-all-start = ((bf16[16,3,160,128]{3,2,1,0:T(8,128)(2,1)}), bf16[16,3,160,128]{3,2,1,0:T(8,128)(2,1)S(1)}, u32[]{:S(2)}, u32[]{:S(2)}) async-start(bf16[16,3,160,128]{3,2,1,0:T(8,128)(2,1)} %pack.1), calls=%async_computation | async-start | bytes 3932160 | tf_op jit(solution)/shard_map/all_to_all | solution.py:242
  10.1 3.9 %split.1 = (bf16[3,160,128]{2,1,0:T(8,128)(2,1)}, bf16[3,160,128]{2,1,0:T(8,128)(2,1)}, bf16[3,160,128]{2,1,0:T(8,128)(2,1)}, bf16[3,160,128]{2,1,0:T(8,128)(2,1...) custom-call(s32[1]{0:T(128)} %bitcast.1.me_ref, ...), custom_call_target="tpu_custom_call" | custom-call | tf_op jit(solution)/shard_map/split/pallas_call | solution.py:198
  14.0 0.1 collective-permute-start
  14.1 1.6 %collective-permute-start.1 = (bf16[3,160,128]{2,1,0:T(8,128)(2,1)}, bf16[3,160,128]{2,1,0:T(8,128)(2,1)S(1)}, u32[]{:S(2)}, u32[]{:S(2)}) collective-permute-start(bf16[3,160,128]{2,1,0:T(8,128)(2,1)} %get-tuple-element.23), channel_id=1, source_target_pairs={{0,2},{1,3},{2,0},{3,1},{4,6},{5,7},{6,4},{7,5},{8,10},{9,11},{10,... | collective-permute-start | bytes 368648 | tf_op jit(solution)/shard_map/ppermute | solution.py:249
  15.8 0.4 collective-permute-start.2
  16.2 1.4 collective-permute-start.3
  17.5 0.3 collective-permute-start.4
  17.8 0.0 collective-permute-done.refs_1_
  17.8 2.4 %collective-permute-start.5 = (bf16[3,160,128]{2,1,0:T(8,128)(2,1)}, bf16[3,160,128]{2,1,0:T(8,128)(2,1)S(1)}, u32[]{:S(2)}, u32[]{:S(2)}) collective-permute-start(bf16[3,160,128]{2,1,0:T(8,128)(2,1)} %get-tuple-element.27), channel_id=1, source_target_pairs={{0,6},{1,7},{2,4},{3,5},{4,2},{5,3},{6,0},{7,1},{8,14},{9,15},{10,... | collective-permute-start | bytes 368648 | tf_op jit(solution)/shard_map/ppermute | solution.py:249
  20.2 6.4 %collective-permute-done.1.refs_2_ = bf16[3,160,128]{2,1,0:T(8,128)(2,1)S(1)} collective-permute-done((bf16[3,160,128]{2,1,0:T(8,128)(2,1)}, bf16[3,160,128]{2,1,0:T(8,128)(2,1)S(1)}, u32[]{:S(2)}, u32[]{:S(2)}) %collective-permute-start.1) | collective-permute-done | bytes 122912 | tf_op jit(solution)/shard_map/ppermute | solution.py:249
  26.6 1.6 collective-permute-start.6
  28.2 5.3 %collective-permute-done.2.refs_3_ = bf16[3,160,128]{2,1,0:T(8,128)(2,1)S(1)} collective-permute-done((bf16[3,160,128]{2,1,0:T(8,128)(2,1)}, bf16[3,160,128]{2,1,0:T(8,128)(2,1)S(1)}, u32[]{:S(2)}, u32[]{:S(2)}) %collective-permute-start.2) | collective-permute-done | bytes 122912 | tf_op jit(solution)/shard_map/ppermute | solution.py:249
  33.5 0.0 collective-permute-start.7
  33.5 11.8 %collective-permute-done.3.refs_4_ = bf16[3,160,128]{2,1,0:T(8,128)(2,1)S(1)} collective-permute-done((bf16[3,160,128]{2,1,0:T(8,128)(2,1)}, bf16[3,160,128]{2,1,0:T(8,128)(2,1)S(1)}, u32[]{:S(2)}, u32[]{:S(2)}) %collective-permute-start.3) | collective-permute-done | bytes 122912 | tf_op jit(solution)/shard_map/ppermute | solution.py:249
  45.3 5.0 %collective-permute-start.8 = (bf16[3,160,128]{2,1,0:T(8,128)(2,1)}, bf16[3,160,128]{2,1,0:T(8,128)(2,1)S(1)}, u32[]{:S(2)}, u32[]{:S(2)}) collective-permute-start(bf16[3,160,128]{2,1,0:T(8,128)(2,1)} %get-tuple-element.30), channel_id=1, source_target_pairs={{0,9},{1,8},{2,11},{3,10},{4,13},{5,12},{6,15},{7,14},{8,1},{9,0},... | collective-permute-start | bytes 368648 | tf_op jit(solution)/shard_map/ppermute | solution.py:249
  50.3 0.0 collective-permute-done.4.refs_5_
  50.3 3.4 %collective-permute-start.9 = (bf16[3,160,128]{2,1,0:T(8,128)(2,1)}, bf16[3,160,128]{2,1,0:T(8,128)(2,1)S(1)}, u32[]{:S(2)}, u32[]{:S(2)}) collective-permute-start(bf16[3,160,128]{2,1,0:T(8,128)(2,1)} %get-tuple-element.31), channel_id=1, source_target_pairs={{0,10},{1,11},{2,8},{3,9},{4,14},{5,15},{6,12},{7,13},{8,2},{9,3},... | collective-permute-start | bytes 368648 | tf_op jit(solution)/shard_map/ppermute | solution.py:249
  53.7 0.0 collective-permute-done.5.refs_6_
  53.7 2.8 %collective-permute-start.10 = (bf16[3,160,128]{2,1,0:T(8,128)(2,1)}, bf16[3,160,128]{2,1,0:T(8,128)(2,1)S(1)}, u32[]{:S(2)}, u32[]{:S(2)}) collective-permute-start(bf16[3,160,128]{2,1,0:T(8,128)(2,1)} %get-tuple-element.32), channel_id=1, source_target_pairs={{0,11},{1,10},{2,9},{3,8},{4,15},{5,14},{6,13},{7,12},{8,3},{9,2},... | collective-permute-start | bytes 368648 | tf_op jit(solution)/shard_map/ppermute | solution.py:249
  56.5 0.0 collective-permute-done.6.refs_7_
  56.5 1.3 collective-permute-start.11
  57.8 14.4 %collective-permute-done.7.refs_8_ = bf16[3,160,128]{2,1,0:T(8,128)(2,1)S(1)} collective-permute-done((bf16[3,160,128]{2,1,0:T(8,128)(2,1)}, bf16[3,160,128]{2,1,0:T(8,128)(2,1)S(1)}, u32[]{:S(2)}, u32[]{:S(2)}) %collective-permute-start.7) | collective-permute-done | bytes 122912 | tf_op jit(solution)/shard_map/ppermute | solution.py:249
  72.2 1.8 %collective-permute-start.12 = (bf16[3,160,128]{2,1,0:T(8,128)(2,1)}, bf16[3,160,128]{2,1,0:T(8,128)(2,1)}, u32[]{:S(2)}, u32[]{:S(2)}) collective-permute-start(bf16[3,160,128]{2,1,0:T(8,128)(2,1)} %get-tuple-element.34), channel_id=1, source_target_pairs={{0,13},{1,12},{2,15},{3,14},{4,9},{5,8},{6,11},{7,10},{8,5},{9,4},... | collective-permute-start | bytes 368648 | tf_op jit(solution)/shard_map/ppermute | solution.py:249
  74.0 1.6 %collective-permute-done.8.refs_9_ = bf16[3,160,128]{2,1,0:T(8,128)(2,1)S(1)} collective-permute-done((bf16[3,160,128]{2,1,0:T(8,128)(2,1)}, bf16[3,160,128]{2,1,0:T(8,128)(2,1)S(1)}, u32[]{:S(2)}, u32[]{:S(2)}) %collective-permute-start.8) | collective-permute-done | bytes 122912 | tf_op jit(solution)/shard_map/ppermute | solution.py:249
  75.7 2.6 %collective-permute-start.13 = (bf16[3,160,128]{2,1,0:T(8,128)(2,1)}, bf16[3,160,128]{2,1,0:T(8,128)(2,1)}, u32[]{:S(2)}, u32[]{:S(2)}) collective-permute-start(bf16[3,160,128]{2,1,0:T(8,128)(2,1)} %get-tuple-element.35), channel_id=1, source_target_pairs={{0,14},{1,15},{2,12},{3,13},{4,10},{5,11},{6,8},{7,9},{8,6},{9,7},... | collective-permute-start | bytes 368648 | tf_op jit(solution)/shard_map/ppermute | solution.py:249
  78.2 2.7 %collective-permute-done.9.refs_10_ = bf16[3,160,128]{2,1,0:T(8,128)(2,1)S(1)} collective-permute-done((bf16[3,160,128]{2,1,0:T(8,128)(2,1)}, bf16[3,160,128]{2,1,0:T(8,128)(2,1)S(1)}, u32[]{:S(2)}, u32[]{:S(2)}) %collective-permute-start.9) | collective-permute-done | bytes 122912 | tf_op jit(solution)/shard_map/ppermute | solution.py:249
  80.9 1.9 %collective-permute-start.14 = (bf16[3,160,128]{2,1,0:T(8,128)(2,1)}, bf16[3,160,128]{2,1,0:T(8,128)(2,1)}, u32[]{:S(2)}, u32[]{:S(2)}) collective-permute-start(bf16[3,160,128]{2,1,0:T(8,128)(2,1)} %get-tuple-element.36), channel_id=1, source_target_pairs={{0,15},{1,14},{2,13},{3,12},{4,11},{5,10},{6,9},{7,8},{8,7},{9,6},... | collective-permute-start | bytes 368648 | tf_op jit(solution)/shard_map/ppermute | solution.py:249
  82.8 5.6 %collective-permute-done.10.refs_11_ = bf16[3,160,128]{2,1,0:T(8,128)(2,1)S(1)} collective-permute-done((bf16[3,160,128]{2,1,0:T(8,128)(2,1)}, bf16[3,160,128]{2,1,0:T(8,128)(2,1)S(1)}, u32[]{:S(2)}, u32[]{:S(2)}) %collective-permute-start.10) | collective-permute-done | bytes 122912 | tf_op jit(solution)/shard_map/ppermute | solution.py:249
  88.4 0.0 collective-permute-done.11.refs_12_
  88.4 0.0 collective-permute-done.12.refs_13_
  88.4 0.0 collective-permute-done.13.refs_14_
  88.4 0.0 collective-permute-done.14.refs_15_
  88.4 0.0 copy-done.2
  88.4 0.0 copy-done.3
  88.4 0.0 copy-done.4
  88.4 0.0 copy-done.5
  88.5 0.0 copy-done.6
  88.5 0.0 copy-done.7
  88.5 0.5 copy-done.12
  89.0 0.1 copy-done.13
  89.1 14.4 %attend_parts.1 = bf16[2560,128]{1,0:T(8,128)(2,1)} custom-call(s32[5]{0:T(128)} %rank_ref.3, s32[5]{0:T(128)} %ends_ref.3, s32[1]{0:T(128)} %bitcast.1.me_ref, bf16[3,160,128]{2,1,0:T(8,128)(2,1)} %get-tuple-element.21.refs_0_, bf16[3,160,128]{2,1,0:T(8,128)(2,1)} %copy-done.2, bf16[3,160,128]{2,1,0:T(8,128)(2,1)} %copy-done.3, ...), custom_call_target="tpu_custom_call" | custom-call | tf_op jit(solution)/shard_map/attend_parts/pallas_call | solution.py:138
  103.5 0.0 all-to-all-done.q_ref.kf_ref.vf_ref
  103.5 13.0 %all-to-all-start.2 = ((bf16[16,160,128]{2,1,0:T(8,128)(2,1)}), bf16[16,160,128]{2,1,0:T(8,128)(2,1)S(1)}, u32[]{:S(2)}, u32[]{:S(2)}) async-start(bf16[16,160,128]{2,1,0:T(8,128)(2,1)} %bitcast.4), calls=%async_computation.2 | async-start | bytes 1310720 | tf_op jit(solution)/shard_map/all_to_all | solution.py:242
  116.6 14.2 %attend_whole.1 = bf16[2560,128]{1,0:T(8,128)(2,1)} custom-call(s32[5]{0:T(128)} %rank_ref.3, s32[5]{0:T(128)} %ends_ref.3, bf16[16,3,160,128]{3,2,1,0:T(8,128)(2,1)} %copy-done, bf16[16,3,160,128]{3,2,1,0:T(8,128)(2,1)} %copy-done, bf16[16,3,160,128]{3,2,1,0:T(8,128)(2,1)} %copy-done, bf16[2560,256]{1,0:T(8,128)(2,1)} %refs_16_.1, bf16[2560,256]{1,0:T(8,128)(2,1)} %refs_17_.1), custom_call_target="tpu_custom_call" | custom-call | tf_op jit(solution)/shard_map/attend_whole/pallas_call | solution.py:108
  130.7 2.1 %all-to-all-done.2.refs_1_ = bf16[16,160,128]{2,1,0:T(8,128)(2,1)S(1)} async-done(((bf16[16,160,128]{2,1,0:T(8,128)(2,1)}), bf16[16,160,128]{2,1,0:T(8,128)(2,1)S(1)}, u32[]{:S(2)}, u32[]{:S(2)}) %all-to-all-start.2) | async-done | bytes 655392 | tf_op jit(solution)/shard_map/all_to_all | solution.py:242
  132.9 23.4 %all_to_all.15.refs_0_ = bf16[16,160,128]{2,1,0:T(8,128)(2,1)} all-to-all(bf16[16,160,128]{2,1,0:T(8,128)(2,1)} %bitcast.3), channel_id=1, replica_groups=mesh['groups'=2,'seq'=16] {'seq'}, dimensions={0} | all-to-all | bytes 1310720 | tf_op jit(solution)/shard_map/all_to_all | solution.py:242
  156.2 2.3 %unpack.1 = bf16[160,4096]{1,0:T(8,128)(2,1)} custom-call(bf16[16,160,128]{2,1,0:T(8,128)(2,1)} %all_to_all.15.refs_0_, bf16[16,160,128]{2,1,0:T(8,128)(2,1)} %copy-done.1), custom_call_target="tpu_custom_call" | custom-call | tf_op jit(solution)/shard_map/unpack/pallas_call | solution.py:224
  (20 shorter events, 0.0 us)
Async XLA Ops:
  2.8 100.7 %all-to-all-start = ((bf16[16,3,160,128]{3,2,1,0:T(8,128)(2,1)}), bf16[16,3,160,128]{3,2,1,0:T(8,128)(2,1)S(1)}, u32[]{:S(2)}, u32[]{:S(2)}) async-start(bf16[16,3,160,128]{3,2,1,0:T(8,128)(2,1)} %pack.1), calls=%async_computation | async-start | bytes 3932160 | tf_op jit(solution)/shard_map/all_to_all | solution.py:242
  14.0 3.8 %collective-permute-start = (bf16[3,160,128]{2,1,0:T(8,128)(2,1)}, bf16[3,160,128]{2,1,0:T(8,128)(2,1)S(1)}, u32[]{:S(2)}, u32[]{:S(2)}) collective-permute-start(bf16[3,160,128]{2,1,0:T(8,128)(2,1)} %get-tuple-element.22), channel_id=1, source_target_pairs={{0,1},{1,0},{2,3},{3,2},{4,5},{5,4},{6,7},{7,6},{8,9},{9,8},{10,11... | collective-permute-start | bytes 368648 | tf_op jit(solution)/shard_map/ppermute | solution.py:249
  14.1 12.5 %collective-permute-start.1 = (bf16[3,160,128]{2,1,0:T(8,128)(2,1)}, bf16[3,160,128]{2,1,0:T(8,128)(2,1)S(1)}, u32[]{:S(2)}, u32[]{:S(2)}) collective-permute-start(bf16[3,160,128]{2,1,0:T(8,128)(2,1)} %get-tuple-element.23), channel_id=1, source_target_pairs={{0,2},{1,3},{2,0},{3,1},{4,6},{5,7},{6,4},{7,5},{8,10},{9,11},{10,... | collective-permute-start | bytes 368648 | tf_op jit(solution)/shard_map/ppermute | solution.py:249
  15.8 17.7 %collective-permute-start.2 = (bf16[3,160,128]{2,1,0:T(8,128)(2,1)}, bf16[3,160,128]{2,1,0:T(8,128)(2,1)S(1)}, u32[]{:S(2)}, u32[]{:S(2)}) collective-permute-start(bf16[3,160,128]{2,1,0:T(8,128)(2,1)} %get-tuple-element.24), channel_id=1, source_target_pairs={{0,3},{1,2},{2,1},{3,0},{4,7},{5,6},{6,5},{7,4},{8,11},{9,10},{10,... | collective-permute-start | bytes 368648 | tf_op jit(solution)/shard_map/ppermute | solution.py:249
  16.2 29.1 %collective-permute-start.3 = (bf16[3,160,128]{2,1,0:T(8,128)(2,1)}, bf16[3,160,128]{2,1,0:T(8,128)(2,1)S(1)}, u32[]{:S(2)}, u32[]{:S(2)}) collective-permute-start(bf16[3,160,128]{2,1,0:T(8,128)(2,1)} %get-tuple-element.25), channel_id=1, source_target_pairs={{0,4},{1,5},{2,6},{3,7},{4,0},{5,1},{6,2},{7,3},{8,12},{9,13},{10,... | collective-permute-start | bytes 368648 | tf_op jit(solution)/shard_map/ppermute | solution.py:249
  17.5 32.8 %collective-permute-start.4 = (bf16[3,160,128]{2,1,0:T(8,128)(2,1)}, bf16[3,160,128]{2,1,0:T(8,128)(2,1)S(1)}, u32[]{:S(2)}, u32[]{:S(2)}) collective-permute-start(bf16[3,160,128]{2,1,0:T(8,128)(2,1)} %get-tuple-element.26), channel_id=1, source_target_pairs={{0,5},{1,4},{2,7},{3,6},{4,1},{5,0},{6,3},{7,2},{8,13},{9,12},{10,... | collective-permute-start | bytes 368648 | tf_op jit(solution)/shard_map/ppermute | solution.py:249
  17.8 70.6 %copy-start.2 = (bf16[3,160,128]{2,1,0:T(8,128)(2,1)}, bf16[3,160,128]{2,1,0:T(8,128)(2,1)S(1)}, u32[]{:S(2)}) copy-start(bf16[3,160,128]{2,1,0:T(8,128)(2,1)S(1)} %collective-permute-done.refs_1_) | copy-start | bytes 368644
  17.8 35.9 %collective-permute-start.5 = (bf16[3,160,128]{2,1,0:T(8,128)(2,1)}, bf16[3,160,128]{2,1,0:T(8,128)(2,1)S(1)}, u32[]{:S(2)}, u32[]{:S(2)}) collective-permute-start(bf16[3,160,128]{2,1,0:T(8,128)(2,1)} %get-tuple-element.27), channel_id=1, source_target_pairs={{0,6},{1,7},{2,4},{3,5},{4,2},{5,3},{6,0},{7,1},{8,14},{9,15},{10,... | collective-permute-start | bytes 368648 | tf_op jit(solution)/shard_map/ppermute | solution.py:249
  26.6 61.8 %copy-start.3 = (bf16[3,160,128]{2,1,0:T(8,128)(2,1)}, bf16[3,160,128]{2,1,0:T(8,128)(2,1)S(1)}, u32[]{:S(2)}) copy-start(bf16[3,160,128]{2,1,0:T(8,128)(2,1)S(1)} %collective-permute-done.1.refs_2_) | copy-start | bytes 368644
  26.6 29.9 %collective-permute-start.6 = (bf16[3,160,128]{2,1,0:T(8,128)(2,1)}, bf16[3,160,128]{2,1,0:T(8,128)(2,1)S(1)}, u32[]{:S(2)}, u32[]{:S(2)}) collective-permute-start(bf16[3,160,128]{2,1,0:T(8,128)(2,1)} %get-tuple-element.28), channel_id=1, source_target_pairs={{0,7},{1,6},{2,5},{3,4},{4,3},{5,2},{6,1},{7,0},{8,15},{9,14},{10,... | collective-permute-start | bytes 368648 | tf_op jit(solution)/shard_map/ppermute | solution.py:249
  33.5 55.0 %copy-start.4 = (bf16[3,160,128]{2,1,0:T(8,128)(2,1)}, bf16[3,160,128]{2,1,0:T(8,128)(2,1)S(1)}, u32[]{:S(2)}) copy-start(bf16[3,160,128]{2,1,0:T(8,128)(2,1)S(1)} %collective-permute-done.2.refs_3_) | copy-start | bytes 368644
  33.5 38.7 %collective-permute-start.7 = (bf16[3,160,128]{2,1,0:T(8,128)(2,1)}, bf16[3,160,128]{2,1,0:T(8,128)(2,1)S(1)}, u32[]{:S(2)}, u32[]{:S(2)}) collective-permute-start(bf16[3,160,128]{2,1,0:T(8,128)(2,1)} %get-tuple-element.29), channel_id=1, source_target_pairs={{0,8},{1,9},{2,10},{3,11},{4,12},{5,13},{6,14},{7,15},{8,0},{9,1},... | collective-permute-start | bytes 368648 | tf_op jit(solution)/shard_map/ppermute | solution.py:249
  45.3 43.2 %copy-start.5 = (bf16[3,160,128]{2,1,0:T(8,128)(2,1)}, bf16[3,160,128]{2,1,0:T(8,128)(2,1)S(1)}, u32[]{:S(2)}) copy-start(bf16[3,160,128]{2,1,0:T(8,128)(2,1)S(1)} %collective-permute-done.3.refs_4_) | copy-start | bytes 368644
  45.3 30.4 %collective-permute-start.8 = (bf16[3,160,128]{2,1,0:T(8,128)(2,1)}, bf16[3,160,128]{2,1,0:T(8,128)(2,1)S(1)}, u32[]{:S(2)}, u32[]{:S(2)}) collective-permute-start(bf16[3,160,128]{2,1,0:T(8,128)(2,1)} %get-tuple-element.30), channel_id=1, source_target_pairs={{0,9},{1,8},{2,11},{3,10},{4,13},{5,12},{6,15},{7,14},{8,1},{9,0},... | collective-permute-start | bytes 368648 | tf_op jit(solution)/shard_map/ppermute | solution.py:249
  50.3 38.1 %copy-start.6 = (bf16[3,160,128]{2,1,0:T(8,128)(2,1)}, bf16[3,160,128]{2,1,0:T(8,128)(2,1)S(1)}, u32[]{:S(2)}) copy-start(bf16[3,160,128]{2,1,0:T(8,128)(2,1)S(1)} %collective-permute-done.4.refs_5_) | copy-start | bytes 368644
  50.3 30.6 %collective-permute-start.9 = (bf16[3,160,128]{2,1,0:T(8,128)(2,1)}, bf16[3,160,128]{2,1,0:T(8,128)(2,1)S(1)}, u32[]{:S(2)}, u32[]{:S(2)}) collective-permute-start(bf16[3,160,128]{2,1,0:T(8,128)(2,1)} %get-tuple-element.31), channel_id=1, source_target_pairs={{0,10},{1,11},{2,8},{3,9},{4,14},{5,15},{6,12},{7,13},{8,2},{9,3},... | collective-permute-start | bytes 368648 | tf_op jit(solution)/shard_map/ppermute | solution.py:249
  53.7 34.8 %copy-start.7 = (bf16[3,160,128]{2,1,0:T(8,128)(2,1)}, bf16[3,160,128]{2,1,0:T(8,128)(2,1)S(1)}, u32[]{:S(2)}) copy-start(bf16[3,160,128]{2,1,0:T(8,128)(2,1)S(1)} %collective-permute-done.5.refs_6_) | copy-start | bytes 368644
  53.7 34.7 %collective-permute-start.10 = (bf16[3,160,128]{2,1,0:T(8,128)(2,1)}, bf16[3,160,128]{2,1,0:T(8,128)(2,1)S(1)}, u32[]{:S(2)}, u32[]{:S(2)}) collective-permute-start(bf16[3,160,128]{2,1,0:T(8,128)(2,1)} %get-tuple-element.32), channel_id=1, source_target_pairs={{0,11},{1,10},{2,9},{3,8},{4,15},{5,14},{6,13},{7,12},{8,3},{9,2},... | collective-permute-start | bytes 368648 | tf_op jit(solution)/shard_map/ppermute | solution.py:249
  56.5 32.0 %copy-start.8 = (bf16[3,160,128]{2,1,0:T(8,128)(2,1)}, bf16[3,160,128]{2,1,0:T(8,128)(2,1)S(1)}, u32[]{:S(2)}) copy-start(bf16[3,160,128]{2,1,0:T(8,128)(2,1)S(1)} %collective-permute-done.6.refs_7_) | copy-start | bytes 368644
  56.5 31.9 %collective-permute-start.11 = (bf16[3,160,128]{2,1,0:T(8,128)(2,1)}, bf16[3,160,128]{2,1,0:T(8,128)(2,1)S(1)}, u32[]{:S(2)}, u32[]{:S(2)}) collective-permute-start(bf16[3,160,128]{2,1,0:T(8,128)(2,1)} %get-tuple-element.33), channel_id=1, source_target_pairs={{0,12},{1,13},{2,14},{3,15},{4,8},{5,9},{6,10},{7,11},{8,4},{9,5},... | collective-permute-start | bytes 368648 | tf_op jit(solution)/shard_map/ppermute | solution.py:249
  72.2 16.3 %copy-start.9 = (bf16[3,160,128]{2,1,0:T(8,128)(2,1)}, bf16[3,160,128]{2,1,0:T(8,128)(2,1)S(1)}, u32[]{:S(2)}) copy-start(bf16[3,160,128]{2,1,0:T(8,128)(2,1)S(1)} %collective-permute-done.7.refs_8_) | copy-start | bytes 368644
  72.2 16.2 %collective-permute-start.12 = (bf16[3,160,128]{2,1,0:T(8,128)(2,1)}, bf16[3,160,128]{2,1,0:T(8,128)(2,1)}, u32[]{:S(2)}, u32[]{:S(2)}) collective-permute-start(bf16[3,160,128]{2,1,0:T(8,128)(2,1)} %get-tuple-element.34), channel_id=1, source_target_pairs={{0,13},{1,12},{2,15},{3,14},{4,9},{5,8},{6,11},{7,10},{8,5},{9,4},... | collective-permute-start | bytes 368648 | tf_op jit(solution)/shard_map/ppermute | solution.py:249
  75.7 12.8 %copy-start.10 = (bf16[3,160,128]{2,1,0:T(8,128)(2,1)}, bf16[3,160,128]{2,1,0:T(8,128)(2,1)S(1)}, u32[]{:S(2)}) copy-start(bf16[3,160,128]{2,1,0:T(8,128)(2,1)S(1)} %collective-permute-done.8.refs_9_) | copy-start | bytes 368644
  75.7 12.7 %collective-permute-start.13 = (bf16[3,160,128]{2,1,0:T(8,128)(2,1)}, bf16[3,160,128]{2,1,0:T(8,128)(2,1)}, u32[]{:S(2)}, u32[]{:S(2)}) collective-permute-start(bf16[3,160,128]{2,1,0:T(8,128)(2,1)} %get-tuple-element.35), channel_id=1, source_target_pairs={{0,14},{1,15},{2,12},{3,13},{4,10},{5,11},{6,8},{7,9},{8,6},{9,7},... | collective-permute-start | bytes 368648 | tf_op jit(solution)/shard_map/ppermute | solution.py:249
  80.9 7.6 %copy-start.11 = (bf16[3,160,128]{2,1,0:T(8,128)(2,1)}, bf16[3,160,128]{2,1,0:T(8,128)(2,1)S(1)}, u32[]{:S(2)}) copy-start(bf16[3,160,128]{2,1,0:T(8,128)(2,1)S(1)} %collective-permute-done.9.refs_10_) | copy-start | bytes 368644
  80.9 7.5 %collective-permute-start.14 = (bf16[3,160,128]{2,1,0:T(8,128)(2,1)}, bf16[3,160,128]{2,1,0:T(8,128)(2,1)}, u32[]{:S(2)}, u32[]{:S(2)}) collective-permute-start(bf16[3,160,128]{2,1,0:T(8,128)(2,1)} %get-tuple-element.36), channel_id=1, source_target_pairs={{0,15},{1,14},{2,13},{3,12},{4,11},{5,10},{6,9},{7,8},{8,7},{9,6},... | collective-permute-start | bytes 368648 | tf_op jit(solution)/shard_map/ppermute | solution.py:249
  88.4 0.7 copy-start.12
  88.4 0.7 copy-start.13
  103.5 13.0 %copy-start = (bf16[16,3,160,128]{3,2,1,0:T(8,128)(2,1)}, bf16[16,3,160,128]{3,2,1,0:T(8,128)(2,1)S(1)}, u32[]{:S(2)}) copy-start(bf16[16,3,160,128]{3,2,1,0:T(8,128)(2,1)S(1)} %all-to-all-done.q_ref.kf_ref.vf_ref) | copy-start | bytes 5898244
  103.5 29.3 %all-to-all-start.2 = ((bf16[16,160,128]{2,1,0:T(8,128)(2,1)}), bf16[16,160,128]{2,1,0:T(8,128)(2,1)S(1)}, u32[]{:S(2)}, u32[]{:S(2)}) async-start(bf16[16,160,128]{2,1,0:T(8,128)(2,1)} %bitcast.4), calls=%async_computation.2 | async-start | bytes 1310720 | tf_op jit(solution)/shard_map/all_to_all | solution.py:242
  132.9 23.4 %copy-start.1 = (bf16[16,160,128]{2,1,0:T(8,128)(2,1)}, bf16[16,160,128]{2,1,0:T(8,128)(2,1)S(1)}, u32[]{:S(2)}) copy-start(bf16[16,160,128]{2,1,0:T(8,128)(2,1)S(1)} %all-to-all-done.2.refs_1_) | copy-start | bytes 1966084

commit v5 on v4

--- a/solution.py
+++ b/solution.py
@@ -91,32 +91,32 @@
 ATTEND_SCRATCH = [pltpu.VMEM((PATCH, PATCH), jnp.float32)] * 2 + [pltpu.VMEM((PATCH, HEAD_DIM), jnp.float32)] * 3
 
 
-def attend_whole_kernel(rank_ref, ends_ref, q_ref, kf_ref, vf_ref, ks_ref, vs_ref, out_ref, *scratch):
-    flat = (q_ref.shape[0] * q_ref.shape[1], HEAD_DIM)
-    fresh = [ref.reshape(*flat) for ref in (q_ref, kf_ref, vf_ref)]
+def attend_whole_kernel(rank_ref, ends_ref, packed_ref, ks_ref, vs_ref, out_ref, *refs):
+    fresh, scratch = refs[:3], refs[3:]
+    peers, _, rows_here, _ = packed_ref.shape
+    for t in range(peers):
+        for i, ref in enumerate(fresh):
+            ref[t * rows_here:(t + 1) * rows_here, :] = packed_ref[t, i]
     attend_all(rank_ref, ends_ref, *fresh, ks_ref, vs_ref, out_ref, scratch)
 
 
 def attend_whole(packed, k_stale, v_stale, rank, ends, head):
-    shards_here, _, rows_here, _ = packed.shape
-    total_rows = shards_here * rows_here
-    part = [
-        pl.BlockSpec((shards_here, None, rows_here, HEAD_DIM), lambda p, r, e, i=i: (0, i, 0, 0))
-        for i in range(3)
-    ]
+    peers, _, rows_here, _ = packed.shape
+    total_rows = peers * rows_here
     stale = pl.BlockSpec((total_rows, HEAD_DIM), lambda p, r, e: (0, head))
     return pl.pallas_call(
         attend_whole_kernel,
         grid_spec=pltpu.PrefetchScalarGridSpec(
             num_scalar_prefetch=2,
             grid=(1,),
-            in_specs=[*part, stale, stale],
+            in_specs=[pl.BlockSpec(memory_space=pltpu.VMEM), stale, stale],
             out_specs=pl.BlockSpec((total_rows, HEAD_DIM), lambda p, r, e: (0, 0)),
-            scratch_shapes=ATTEND_SCRATCH,
+            scratch_shapes=[pltpu.VMEM((total_rows, HEAD_DIM), jnp.bfloat16)] * 3 + ATTEND_SCRATCH,
         ),
         out_shape=jax.ShapeDtypeStruct((total_rows, HEAD_DIM), jnp.bfloat16),
+        compiler_params=pltpu.CompilerParams(vmem_limit_bytes=61 << 20),
         name="attend_whole",
-    )(rank, ends, packed, packed, packed, k_stale, v_stale)
+    )(rank, ends, packed, k_stale, v_stale)
 
 
 def attend_parts_kernel(rank_ref, ends_ref, me_ref, *refs, peers):
@@ -140,11 +140,12 @@
         grid_spec=pltpu.PrefetchScalarGridSpec(
             num_scalar_prefetch=3,
             grid=(1,),
-            in_specs=[pl.BlockSpec(blocks[0].shape, lambda p, r, e, m: (0, 0, 0))] * peers + [stale, stale],
+            in_specs=[pl.BlockSpec(memory_space=pltpu.VMEM)] * peers + [stale, stale],
             out_specs=pl.BlockSpec((total_rows, HEAD_DIM), lambda p, r, e, m: (0, 0)),
             scratch_shapes=[pltpu.VMEM((total_rows, HEAD_DIM), jnp.bfloat16)] * 3 + ATTEND_SCRATCH,
         ),
         out_shape=jax.ShapeDtypeStruct((total_rows, HEAD_DIM), jnp.bfloat16),
+        compiler_params=pltpu.CompilerParams(vmem_limit_bytes=24 << 20),
         name="attend_parts",
     )(rank, ends, me, *blocks, k_stale, v_stale)
 
@@ -204,6 +205,7 @@
             out_specs=[pl.BlockSpec(shape, lambda g, m: (0, 0, 0))] * peers,
         ),
         out_shape=[jax.ShapeDtypeStruct(shape, jnp.bfloat16)] * peers,
+        compiler_params=pltpu.CompilerParams(vmem_limit_bytes=24 << 20),
         name="split",
     )(me, *arrays)
 
@@ -227,6 +229,7 @@
         in_specs=[pl.BlockSpec((each, rows_here, HEAD_DIM), lambda g: (g, 0, 0))] * heads_here,
         out_specs=pl.BlockSpec((rows_here, each * heads_here * HEAD_DIM), lambda g: (0, g)),
         out_shape=jax.ShapeDtypeStruct((rows_here, others * heads_here * HEAD_DIM), jnp.bfloat16),
+        compiler_params=pltpu.CompilerParams(vmem_limit_bytes=24 << 20),
         name="unpack",
     )(*returned)
 

time: 159 us -> 156 us (0.981)
  Pallas kernels: 37.6 us -> 31.4 us
  waiting for transfers between devices: 50 us -> 51.8 us
    pallas_call x1, Pallas kernels: 3.86 us -> 0.52 us  [split(): pl.pallas_call(functools.partial(split_kernel, head=head, heads_here=head...]
    ppermute x15, waiting for transfers between devices: 47.9 us -> 49.8 us  [shards(): lax.ppermute(blocks[k], 'seq', [(s, s ^ k) for s in range(peers)])]
    pallas_call x1, Pallas kernels: 14.4 us -> 12.6 us  [attend_parts(): pl.pallas_call(functools.partial(attend_parts_kernel, peers=peers), grid_...]
  transfers between devices with their start and end apart: 17 -> 17, of which waited for: 8 -> 8; matrix products, arithmetic and copies ran while one was open for 0% -> 0% of each run, Pallas kernels for 20% -> 18%
where the time goes in v5:
time: 156 us; the launch traced here: 155 us
  waiting for transfers between devices  51.8 us (33%)
  starting transfers between devices  47.5 us (30%)
  Pallas kernels  31.4 us (20%)
  blocking collectives  23.3 us (15%)
    ppermute x15, waiting for transfers between devices, shards(): lax.ppermute(blocks[k], 'seq', [(s, s ^ k) for s in range(peers)])  49.8 us
    ppermute x15, starting transfers between devices, shards(): lax.ppermute(blocks[k], 'seq', [(s, s ^ k) for s in range(peers)])  26.6 us
    all_to_all x1, blocking collectives, swap(): return lax.all_to_all(array, 'seq', split_axis=0, concat_axis=0, tiled=True)  23.3 us
    all_to_all x2, starting transfers between devices, swap(): return lax.all_to_all(array, 'seq', split_axis=0, concat_axis=0, tiled=True)  20.9 us
    pallas_call x1, Pallas kernels, attend_whole(): pl.pallas_call(attend_whole_kernel, grid_spec=pltpu.PrefetchScalarGridSpe...  14.3 us
    pallas_call x1, Pallas kernels, attend_parts(): pl.pallas_call(functools.partial(attend_parts_kernel, peers=peers), grid_...  12.6 us
  transfers between devices with their start and end apart: 17, of which 8 were waited for; matrix products, arithmetic and copies ran while one was open for 0% of the time, Pallas kernels for 18%

profile of v5, /device:TPU:1, one launch (start us, length us, event | category | flops | bytes accessed | tf_op | source)
XLA Modules:
  0.0 155.4 jit_solution(5759428006115552629)
XLA Ops:
  0.0 2.8 %pack.1 = bf16[16,3,160,128]{3,2,1,0:T(8,128)(2,1)} custom-call(bf16[160,4096]{1,0:T(8,128)(2,1)} %q_ref.3, bf16[160,4096]{1,0:T(8,128)(2,1)} %k_ref.3, bf16[160,4096]{1,0:T(8,128)(2,1)} %v_ref.3), custom_call_target="tpu_custom_call" | custom-call | tf_op jit(solution)/shard_map/pack/pallas_call | solution.py:175
  2.8 0.0 copy-start
  2.8 0.0 copy-start.1
  2.8 7.5 %all-to-all-start = ((bf16[16,3,160,128]{3,2,1,0:T(8,128)(2,1)}), bf16[16,3,160,128]{3,2,1,0:T(8,128)(2,1)}, u32[]{:S(2)}, u32[]{:S(2)}) async-start(bf16[16,3,160,128]{3,2,1,0:T(8,128)(2,1)} %pack.1), calls=%async_computation | async-start | bytes 3932160 | tf_op jit(solution)/shard_map/all_to_all | solution.py:245
  10.3 0.0 copy-done
  10.3 0.0 copy-done.1
  10.3 0.0 copy-start.2
  10.3 1.3 copy-done.2
  11.6 0.5 split.1
  12.2 0.2 collective-permute-start
  12.4 1.6 %collective-permute-start.1 = (bf16[3,160,128]{2,1,0:T(8,128)(2,1)S(1)}, bf16[3,160,128]{2,1,0:T(8,128)(2,1)S(1)}, u32[]{:S(2)}, u32[]{:S(2)}) collective-permute-start(bf16[3,160,128]{2,1,0:T(8,128)(2,1)S(1)} %get-tuple-element.23), channel_id=1, source_target_pairs={{0,2},{1,3},{2,0},{3,1},{4,6},{5,7},{6,4},{7,5},{8,10},{9,11},{10,... | collective-permute-start | bytes 368648 | tf_op jit(solution)/shard_map/ppermute | solution.py:252
  14.0 0.4 collective-permute-start.2
  14.4 1.4 collective-permute-start.3
  15.7 0.3 collective-permute-start.4
  16.0 0.0 collective-permute-done.refs_1_
  16.0 2.4 %collective-permute-start.5 = (bf16[3,160,128]{2,1,0:T(8,128)(2,1)S(1)}, bf16[3,160,128]{2,1,0:T(8,128)(2,1)S(1)}, u32[]{:S(2)}, u32[]{:S(2)}) collective-permute-start(bf16[3,160,128]{2,1,0:T(8,128)(2,1)S(1)} %get-tuple-element.27), channel_id=1, source_target_pairs={{0,6},{1,7},{2,4},{3,5},{4,2},{5,3},{6,0},{7,1},{8,14},{9,15},{10,... | collective-permute-start | bytes 368648 | tf_op jit(solution)/shard_map/ppermute | solution.py:252
  18.4 8.5 %collective-permute-done.1.refs_2_ = bf16[3,160,128]{2,1,0:T(8,128)(2,1)S(1)} collective-permute-done((bf16[3,160,128]{2,1,0:T(8,128)(2,1)S(1)}, bf16[3,160,128]{2,1,0:T(8,128)(2,1)S(1)}, u32[]{:S(2)}, u32[]{:S(2)}) %collective-permute-start.1) | collective-permute-done | bytes 122912 | tf_op jit(solution)/shard_map/ppermute | solution.py:252
  26.8 1.5 collective-permute-start.6
  28.3 5.4 %collective-permute-done.2.refs_3_ = bf16[3,160,128]{2,1,0:T(8,128)(2,1)S(1)} collective-permute-done((bf16[3,160,128]{2,1,0:T(8,128)(2,1)S(1)}, bf16[3,160,128]{2,1,0:T(8,128)(2,1)S(1)}, u32[]{:S(2)}, u32[]{:S(2)}) %collective-permute-start.2) | collective-permute-done | bytes 122912 | tf_op jit(solution)/shard_map/ppermute | solution.py:252
  33.7 0.0 collective-permute-start.7
  33.7 11.6 %collective-permute-done.3.refs_4_ = bf16[3,160,128]{2,1,0:T(8,128)(2,1)S(1)} collective-permute-done((bf16[3,160,128]{2,1,0:T(8,128)(2,1)S(1)}, bf16[3,160,128]{2,1,0:T(8,128)(2,1)S(1)}, u32[]{:S(2)}, u32[]{:S(2)}) %collective-permute-start.3) | collective-permute-done | bytes 122912 | tf_op jit(solution)/shard_map/ppermute | solution.py:252
  45.3 5.1 %collective-permute-start.8 = (bf16[3,160,128]{2,1,0:T(8,128)(2,1)S(1)}, bf16[3,160,128]{2,1,0:T(8,128)(2,1)S(1)}, u32[]{:S(2)}, u32[]{:S(2)}) collective-permute-start(bf16[3,160,128]{2,1,0:T(8,128)(2,1)S(1)} %get-tuple-element.30), channel_id=1, source_target_pairs={{0,9},{1,8},{2,11},{3,10},{4,13},{5,12},{6,15},{7,14},{8,1},{9,0},... | collective-permute-start | bytes 368648 | tf_op jit(solution)/shard_map/ppermute | solution.py:252
  50.5 0.0 collective-permute-done.4.refs_5_
  50.5 3.4 %collective-permute-start.9 = (bf16[3,160,128]{2,1,0:T(8,128)(2,1)S(1)}, bf16[3,160,128]{2,1,0:T(8,128)(2,1)S(1)}, u32[]{:S(2)}, u32[]{:S(2)}) collective-permute-start(bf16[3,160,128]{2,1,0:T(8,128)(2,1)S(1)} %get-tuple-element.31), channel_id=1, source_target_pairs={{0,10},{1,11},{2,8},{3,9},{4,14},{5,15},{6,12},{7,13},{8,2},{9,3},... | collective-permute-start | bytes 368648 | tf_op jit(solution)/shard_map/ppermute | solution.py:252
  53.8 0.0 collective-permute-done.5.refs_6_
  53.9 2.8 %collective-permute-start.10 = (bf16[3,160,128]{2,1,0:T(8,128)(2,1)S(1)}, bf16[3,160,128]{2,1,0:T(8,128)(2,1)S(1)}, u32[]{:S(2)}, u32[]{:S(2)}) collective-permute-start(bf16[3,160,128]{2,1,0:T(8,128)(2,1)S(1)} %get-tuple-element.32), channel_id=1, source_target_pairs={{0,11},{1,10},{2,9},{3,8},{4,15},{5,14},{6,13},{7,12},{8,3},{9,2},... | collective-permute-start | bytes 368648 | tf_op jit(solution)/shard_map/ppermute | solution.py:252
  56.6 0.0 collective-permute-done.6.refs_7_
  56.6 1.3 collective-permute-start.11
  58.0 14.4 %collective-permute-done.7.refs_8_ = bf16[3,160,128]{2,1,0:T(8,128)(2,1)S(1)} collective-permute-done((bf16[3,160,128]{2,1,0:T(8,128)(2,1)S(1)}, bf16[3,160,128]{2,1,0:T(8,128)(2,1)S(1)}, u32[]{:S(2)}, u32[]{:S(2)}) %collective-permute-start.7) | collective-permute-done | bytes 122912 | tf_op jit(solution)/shard_map/ppermute | solution.py:252
  72.3 1.8 %collective-permute-start.12 = (bf16[3,160,128]{2,1,0:T(8,128)(2,1)S(1)}, bf16[3,160,128]{2,1,0:T(8,128)(2,1)S(1)}, u32[]{:S(2)}, u32[]{:S(2)}) collective-permute-start(bf16[3,160,128]{2,1,0:T(8,128)(2,1)S(1)} %get-tuple-element.34), channel_id=1, source_target_pairs={{0,13},{1,12},{2,15},{3,14},{4,9},{5,8},{6,11},{7,10},{8,5},{9,4},... | collective-permute-start | bytes 368648 | tf_op jit(solution)/shard_map/ppermute | solution.py:252
  74.2 1.6 %collective-permute-done.8.refs_9_ = bf16[3,160,128]{2,1,0:T(8,128)(2,1)S(1)} collective-permute-done((bf16[3,160,128]{2,1,0:T(8,128)(2,1)S(1)}, bf16[3,160,128]{2,1,0:T(8,128)(2,1)S(1)}, u32[]{:S(2)}, u32[]{:S(2)}) %collective-permute-start.8) | collective-permute-done | bytes 122912 | tf_op jit(solution)/shard_map/ppermute | solution.py:252
  75.8 2.6 %collective-permute-start.13 = (bf16[3,160,128]{2,1,0:T(8,128)(2,1)S(1)}, bf16[3,160,128]{2,1,0:T(8,128)(2,1)S(1)}, u32[]{:S(2)}, u32[]{:S(2)}) collective-permute-start(bf16[3,160,128]{2,1,0:T(8,128)(2,1)S(1)} %get-tuple-element.35), channel_id=1, source_target_pairs={{0,14},{1,15},{2,12},{3,13},{4,10},{5,11},{6,8},{7,9},{8,6},{9,7},... | collective-permute-start | bytes 368648 | tf_op jit(solution)/shard_map/ppermute | solution.py:252
  78.4 2.7 %collective-permute-done.9.refs_10_ = bf16[3,160,128]{2,1,0:T(8,128)(2,1)S(1)} collective-permute-done((bf16[3,160,128]{2,1,0:T(8,128)(2,1)S(1)}, bf16[3,160,128]{2,1,0:T(8,128)(2,1)S(1)}, u32[]{:S(2)}, u32[]{:S(2)}) %collective-permute-start.9) | collective-permute-done | bytes 122912 | tf_op jit(solution)/shard_map/ppermute | solution.py:252
  81.1 1.9 %collective-permute-start.14 = (bf16[3,160,128]{2,1,0:T(8,128)(2,1)S(1)}, bf16[3,160,128]{2,1,0:T(8,128)(2,1)S(1)}, u32[]{:S(2)}, u32[]{:S(2)}) collective-permute-start(bf16[3,160,128]{2,1,0:T(8,128)(2,1)S(1)} %get-tuple-element.36), channel_id=1, source_target_pairs={{0,15},{1,14},{2,13},{3,12},{4,11},{5,10},{6,9},{7,8},{8,7},{9,6},... | collective-permute-start | bytes 368648 | tf_op jit(solution)/shard_map/ppermute | solution.py:252
  83.0 5.6 %collective-permute-done.10.refs_11_ = bf16[3,160,128]{2,1,0:T(8,128)(2,1)S(1)} collective-permute-done((bf16[3,160,128]{2,1,0:T(8,128)(2,1)S(1)}, bf16[3,160,128]{2,1,0:T(8,128)(2,1)S(1)}, u32[]{:S(2)}, u32[]{:S(2)}) %collective-permute-start.10) | collective-permute-done | bytes 122912 | tf_op jit(solution)/shard_map/ppermute | solution.py:252
  88.5 0.0 collective-permute-done.11.refs_12_
  88.5 0.0 collective-permute-done.12.refs_13_
  88.5 0.0 collective-permute-done.13.refs_14_
  88.5 0.0 collective-permute-done.14.refs_15_
  88.6 0.0 copy-done.3
  88.6 0.0 copy-done.4
  88.6 12.6 %attend_parts.1 = bf16[2560,128]{1,0:T(8,128)(2,1)} custom-call(s32[5]{0:T(128)S(1)} %copy-done.5, s32[5]{0:T(128)S(1)} %copy-done.6, s32[1]{0:T(128)} %bitcast.1.me_ref, bf16[3,160,128]{2,1,0:T(8,128)(2,1)S(1)} %get-tuple-element.21.refs_0_, bf16[3,160,128]{2,1,0:T(8,128)(2,1)S(1)} %collective-permute-done.refs_1_, ...), custom_call_target="tpu_custom_call" | custom-call | tf_op jit(solution)/shard_map/attend_parts/pallas_call | solution.py:138
  101.1 0.0 all-to-all-done.packed_ref
  101.1 13.4 %all-to-all-start.2 = ((bf16[16,160,128]{2,1,0:T(8,128)(2,1)}), bf16[16,160,128]{2,1,0:T(8,128)(2,1)S(1)}, u32[]{:S(2)}, u32[]{:S(2)}) async-start(bf16[16,160,128]{2,1,0:T(8,128)(2,1)} %bitcast.2), calls=%async_computation.2 | async-start | bytes 1310720 | tf_op jit(solution)/shard_map/all_to_all | solution.py:245
  114.6 14.3 %attend_whole.1 = bf16[2560,128]{1,0:T(8,128)(2,1)} custom-call(s32[5]{0:T(128)} %rank_ref.3, s32[5]{0:T(128)} %ends_ref.3, bf16[16,3,160,128]{3,2,1,0:T(8,128)(2,1)} %all-to-all-done.packed_ref, bf16[2560,256]{1,0:T(8,128)(2,1)} %refs_16_.1, bf16[2560,256]{1,0:T(8,128)(2,1)} %refs_17_.1), custom_call_target="tpu_custom_call" | custom-call | tf_op jit(solution)/shard_map/attend_whole/pallas_call | solution.py:107
  128.9 2.0 %all-to-all-done.2.refs_1_ = bf16[16,160,128]{2,1,0:T(8,128)(2,1)S(1)} async-done(((bf16[16,160,128]{2,1,0:T(8,128)(2,1)}), bf16[16,160,128]{2,1,0:T(8,128)(2,1)S(1)}, u32[]{:S(2)}, u32[]{:S(2)}) %all-to-all-start.2) | async-done | bytes 655392 | tf_op jit(solution)/shard_map/all_to_all | solution.py:245
  130.9 23.3 %all_to_all.15.refs_0_ = bf16[16,160,128]{2,1,0:T(8,128)(2,1)S(1)} all-to-all(bf16[16,160,128]{2,1,0:T(8,128)(2,1)} %bitcast.3), channel_id=1, replica_groups=mesh['groups'=2,'seq'=16] {'seq'}, dimensions={0} | all-to-all | bytes 1310720 | tf_op jit(solution)/shard_map/all_to_all | solution.py:245
  154.2 1.2 unpack.1
  (6 shorter events, 0.0 us)
Async XLA Ops:
  2.8 7.5 %copy-start = (bf16[160,4096]{1,0:T(8,128)(2,1)S(1)}, bf16[160,4096]{1,0:T(8,128)(2,1)}, u32[]{:S(2)}) copy-start(bf16[160,4096]{1,0:T(8,128)(2,1)} %q_ref.3) | copy-start | bytes 3932164
  2.8 7.5 %copy-start.1 = (bf16[160,4096]{1,0:T(8,128)(2,1)S(1)}, bf16[160,4096]{1,0:T(8,128)(2,1)}, u32[]{:S(2)}) copy-start(bf16[160,4096]{1,0:T(8,128)(2,1)} %k_ref.3) | copy-start | bytes 3932164
  2.8 98.3 %all-to-all-start = ((bf16[16,3,160,128]{3,2,1,0:T(8,128)(2,1)}), bf16[16,3,160,128]{3,2,1,0:T(8,128)(2,1)}, u32[]{:S(2)}, u32[]{:S(2)}) async-start(bf16[16,3,160,128]{3,2,1,0:T(8,128)(2,1)} %pack.1), calls=%async_computation | async-start | bytes 3932160 | tf_op jit(solution)/shard_map/all_to_all | solution.py:245
  10.3 1.3 copy-start.2
  11.6 76.9 %copy-start.3 = (bf16[2560,256]{1,0:T(8,128)(2,1)S(1)}, bf16[2560,256]{1,0:T(8,128)(2,1)}, u32[]{:S(2)}) copy-start(bf16[2560,256]{1,0:T(8,128)(2,1)} %refs_16_.1) | copy-start | bytes 3932164
  11.6 76.9 %copy-start.4 = (bf16[2560,256]{1,0:T(8,128)(2,1)S(1)}, bf16[2560,256]{1,0:T(8,128)(2,1)}, u32[]{:S(2)}) copy-start(bf16[2560,256]{1,0:T(8,128)(2,1)} %refs_17_.1) | copy-start | bytes 3932164
  11.6 76.9 %copy-start.5 = (s32[5]{0:T(128)S(1)}, s32[5]{0:T(128)}, u32[]{:S(2)}) copy-start(s32[5]{0:T(128)} %rank_ref.3) | copy-start | bytes 64
  11.6 76.9 %copy-start.6 = (s32[5]{0:T(128)S(1)}, s32[5]{0:T(128)}, u32[]{:S(2)}) copy-start(s32[5]{0:T(128)} %ends_ref.3) | copy-start | bytes 64
  12.2 3.8 %collective-permute-start = (bf16[3,160,128]{2,1,0:T(8,128)(2,1)S(1)}, bf16[3,160,128]{2,1,0:T(8,128)(2,1)S(1)}, u32[]{:S(2)}, u32[]{:S(2)}) collective-permute-start(bf16[3,160,128]{2,1,0:T(8,128)(2,1)S(1)} %get-tuple-element.22), channel_id=1, source_target_pairs={{0,1},{1,0},{2,3},{3,2},{4,5},{5,4},{6,7},{7,6},{8,9},{9,8},{10,11... | collective-permute-start | bytes 368648 | tf_op jit(solution)/shard_map/ppermute | solution.py:252
  12.4 14.4 %collective-permute-start.1 = (bf16[3,160,128]{2,1,0:T(8,128)(2,1)S(1)}, bf16[3,160,128]{2,1,0:T(8,128)(2,1)S(1)}, u32[]{:S(2)}, u32[]{:S(2)}) collective-permute-start(bf16[3,160,128]{2,1,0:T(8,128)(2,1)S(1)} %get-tuple-element.23), channel_id=1, source_target_pairs={{0,2},{1,3},{2,0},{3,1},{4,6},{5,7},{6,4},{7,5},{8,10},{9,11},{10,... | collective-permute-start | bytes 368648 | tf_op jit(solution)/shard_map/ppermute | solution.py:252
  14.0 19.7 %collective-permute-start.2 = (bf16[3,160,128]{2,1,0:T(8,128)(2,1)S(1)}, bf16[3,160,128]{2,1,0:T(8,128)(2,1)S(1)}, u32[]{:S(2)}, u32[]{:S(2)}) collective-permute-start(bf16[3,160,128]{2,1,0:T(8,128)(2,1)S(1)} %get-tuple-element.24), channel_id=1, source_target_pairs={{0,3},{1,2},{2,1},{3,0},{4,7},{5,6},{6,5},{7,4},{8,11},{9,10},{10,... | collective-permute-start | bytes 368648 | tf_op jit(solution)/shard_map/ppermute | solution.py:252
  14.4 30.9 %collective-permute-start.3 = (bf16[3,160,128]{2,1,0:T(8,128)(2,1)S(1)}, bf16[3,160,128]{2,1,0:T(8,128)(2,1)S(1)}, u32[]{:S(2)}, u32[]{:S(2)}) collective-permute-start(bf16[3,160,128]{2,1,0:T(8,128)(2,1)S(1)} %get-tuple-element.25), channel_id=1, source_target_pairs={{0,4},{1,5},{2,6},{3,7},{4,0},{5,1},{6,2},{7,3},{8,12},{9,13},{10,... | collective-permute-start | bytes 368648 | tf_op jit(solution)/shard_map/ppermute | solution.py:252
  15.7 34.7 %collective-permute-start.4 = (bf16[3,160,128]{2,1,0:T(8,128)(2,1)S(1)}, bf16[3,160,128]{2,1,0:T(8,128)(2,1)S(1)}, u32[]{:S(2)}, u32[]{:S(2)}) collective-permute-start(bf16[3,160,128]{2,1,0:T(8,128)(2,1)S(1)} %get-tuple-element.26), channel_id=1, source_target_pairs={{0,5},{1,4},{2,7},{3,6},{4,1},{5,0},{6,3},{7,2},{8,13},{9,12},{10,... | collective-permute-start | bytes 368648 | tf_op jit(solution)/shard_map/ppermute | solution.py:252
  16.0 37.8 %collective-permute-start.5 = (bf16[3,160,128]{2,1,0:T(8,128)(2,1)S(1)}, bf16[3,160,128]{2,1,0:T(8,128)(2,1)S(1)}, u32[]{:S(2)}, u32[]{:S(2)}) collective-permute-start(bf16[3,160,128]{2,1,0:T(8,128)(2,1)S(1)} %get-tuple-element.27), channel_id=1, source_target_pairs={{0,6},{1,7},{2,4},{3,5},{4,2},{5,3},{6,0},{7,1},{8,14},{9,15},{10,... | collective-permute-start | bytes 368648 | tf_op jit(solution)/shard_map/ppermute | solution.py:252
  26.8 29.8 %collective-permute-start.6 = (bf16[3,160,128]{2,1,0:T(8,128)(2,1)S(1)}, bf16[3,160,128]{2,1,0:T(8,128)(2,1)S(1)}, u32[]{:S(2)}, u32[]{:S(2)}) collective-permute-start(bf16[3,160,128]{2,1,0:T(8,128)(2,1)S(1)} %get-tuple-element.28), channel_id=1, source_target_pairs={{0,7},{1,6},{2,5},{3,4},{4,3},{5,2},{6,1},{7,0},{8,15},{9,14},{10,... | collective-permute-start | bytes 368648 | tf_op jit(solution)/shard_map/ppermute | solution.py:252
  33.7 38.6 %collective-permute-start.7 = (bf16[3,160,128]{2,1,0:T(8,128)(2,1)S(1)}, bf16[3,160,128]{2,1,0:T(8,128)(2,1)S(1)}, u32[]{:S(2)}, u32[]{:S(2)}) collective-permute-start(bf16[3,160,128]{2,1,0:T(8,128)(2,1)S(1)} %get-tuple-element.29), channel_id=1, source_target_pairs={{0,8},{1,9},{2,10},{3,11},{4,12},{5,13},{6,14},{7,15},{8,0},{9,1},... | collective-permute-start | bytes 368648 | tf_op jit(solution)/shard_map/ppermute | solution.py:252
  45.3 30.5 %collective-permute-start.8 = (bf16[3,160,128]{2,1,0:T(8,128)(2,1)S(1)}, bf16[3,160,128]{2,1,0:T(8,128)(2,1)S(1)}, u32[]{:S(2)}, u32[]{:S(2)}) collective-permute-start(bf16[3,160,128]{2,1,0:T(8,128)(2,1)S(1)} %get-tuple-element.30), channel_id=1, source_target_pairs={{0,9},{1,8},{2,11},{3,10},{4,13},{5,12},{6,15},{7,14},{8,1},{9,0},... | collective-permute-start | bytes 368648 | tf_op jit(solution)/shard_map/ppermute | solution.py:252
  50.5 30.6 %collective-permute-start.9 = (bf16[3,160,128]{2,1,0:T(8,128)(2,1)S(1)}, bf16[3,160,128]{2,1,0:T(8,128)(2,1)S(1)}, u32[]{:S(2)}, u32[]{:S(2)}) collective-permute-start(bf16[3,160,128]{2,1,0:T(8,128)(2,1)S(1)} %get-tuple-element.31), channel_id=1, source_target_pairs={{0,10},{1,11},{2,8},{3,9},{4,14},{5,15},{6,12},{7,13},{8,2},{9,3},... | collective-permute-start | bytes 368648 | tf_op jit(solution)/shard_map/ppermute | solution.py:252
  53.9 34.7 %collective-permute-start.10 = (bf16[3,160,128]{2,1,0:T(8,128)(2,1)S(1)}, bf16[3,160,128]{2,1,0:T(8,128)(2,1)S(1)}, u32[]{:S(2)}, u32[]{:S(2)}) collective-permute-start(bf16[3,160,128]{2,1,0:T(8,128)(2,1)S(1)} %get-tuple-element.32), channel_id=1, source_target_pairs={{0,11},{1,10},{2,9},{3,8},{4,15},{5,14},{6,13},{7,12},{8,3},{9,2},... | collective-permute-start | bytes 368648 | tf_op jit(solution)/shard_map/ppermute | solution.py:252
  56.6 31.9 %collective-permute-start.11 = (bf16[3,160,128]{2,1,0:T(8,128)(2,1)S(1)}, bf16[3,160,128]{2,1,0:T(8,128)(2,1)S(1)}, u32[]{:S(2)}, u32[]{:S(2)}) collective-permute-start(bf16[3,160,128]{2,1,0:T(8,128)(2,1)S(1)} %get-tuple-element.33), channel_id=1, source_target_pairs={{0,12},{1,13},{2,14},{3,15},{4,8},{5,9},{6,10},{7,11},{8,4},{9,5},... | collective-permute-start | bytes 368648 | tf_op jit(solution)/shard_map/ppermute | solution.py:252
  72.3 16.2 %collective-permute-start.12 = (bf16[3,160,128]{2,1,0:T(8,128)(2,1)S(1)}, bf16[3,160,128]{2,1,0:T(8,128)(2,1)S(1)}, u32[]{:S(2)}, u32[]{:S(2)}) collective-permute-start(bf16[3,160,128]{2,1,0:T(8,128)(2,1)S(1)} %get-tuple-element.34), channel_id=1, source_target_pairs={{0,13},{1,12},{2,15},{3,14},{4,9},{5,8},{6,11},{7,10},{8,5},{9,4},... | collective-permute-start | bytes 368648 | tf_op jit(solution)/shard_map/ppermute | solution.py:252
  75.8 12.7 %collective-permute-start.13 = (bf16[3,160,128]{2,1,0:T(8,128)(2,1)S(1)}, bf16[3,160,128]{2,1,0:T(8,128)(2,1)S(1)}, u32[]{:S(2)}, u32[]{:S(2)}) collective-permute-start(bf16[3,160,128]{2,1,0:T(8,128)(2,1)S(1)} %get-tuple-element.35), channel_id=1, source_target_pairs={{0,14},{1,15},{2,12},{3,13},{4,10},{5,11},{6,8},{7,9},{8,6},{9,7},... | collective-permute-start | bytes 368648 | tf_op jit(solution)/shard_map/ppermute | solution.py:252
  81.1 7.5 %collective-permute-start.14 = (bf16[3,160,128]{2,1,0:T(8,128)(2,1)S(1)}, bf16[3,160,128]{2,1,0:T(8,128)(2,1)S(1)}, u32[]{:S(2)}, u32[]{:S(2)}) collective-permute-start(bf16[3,160,128]{2,1,0:T(8,128)(2,1)S(1)} %get-tuple-element.36), channel_id=1, source_target_pairs={{0,15},{1,14},{2,13},{3,12},{4,11},{5,10},{6,9},{7,8},{8,7},{9,6},... | collective-permute-start | bytes 368648 | tf_op jit(solution)/shard_map/ppermute | solution.py:252
  101.1 29.8 %all-to-all-start.2 = ((bf16[16,160,128]{2,1,0:T(8,128)(2,1)}), bf16[16,160,128]{2,1,0:T(8,128)(2,1)S(1)}, u32[]{:S(2)}, u32[]{:S(2)}) async-start(bf16[16,160,128]{2,1,0:T(8,128)(2,1)} %bitcast.2), calls=%async_computation.2 | async-start | bytes 1310720 | tf_op jit(solution)/shard_map/all_to_all | solution.py:245
